TPU v7x, 256 devices: a whole 4x4x8 slice. The times are simulated.
256 devices in a mesh: chan: 64 (over z_lo, y, x), tm: 4 (over z_hi, core).
Axes of the slice: x: 4, y: 4, z: 8 (z_hi: 2, z_lo: 4; z = z_hi * 4 + z_lo), core: 2. Of those that a mesh axis runs over, the one named last changes fastest.
Arguments:
- spectra: bfloat16 [2, 32, 2048, 1024], P(None, 'tm', 'chan'), may hold values from -150 to 150
- quality: int32 [32, 1024], P('tm'), may hold values 0 or 1
- offsets: int32 [4], replicated, may hold values from 1 to 32, as said below
Outputs:
- gathers: float32 [1024, 4, 256], P('chan')
Inputs may be any that keep to these rules, and one draw needn't show every extreme that they name: `offsets`: each offset lies from 1 to 32, and one of them equals 32.
All inputs are finite; a program needn't handle non-finite values. No bound on the sum of `quality` on one device may be relied on, other than what follows from the above.
Results may differ from a plain program's by a relative error of at most 0.0003.
Values may be sent and summed in bfloat16 or wider, within the bound.
A program may use at most 64 MiB of HBM per device.

v0:
```python
import math

import jax
import jax.numpy as jnp
from jax import lax
from jax.sharding import PartitionSpec as P

F = 2048
LAGS = 256
NOFF = 4
CH_DEV = 16
W_DEV = 8


def shifted(value, axis, steps):
    count = lax.axis_size(axis)
    leading, last = (max(0, -steps), min(count, count - steps))
    return lax.ppermute(value, axis, [(source, source + steps) for source in range(leading, last)])


def lag_table(freq_count, lag_count):
    freq_index = jnp.arange(freq_count, dtype=jnp.int32)[:, None]
    double_lag = (2 * jnp.arange(lag_count, dtype=jnp.int32) - lag_count + 1)[None, :]
    turns = jnp.mod(freq_index * double_lag, 4 * freq_count)
    angles = turns.astype(jnp.float32) * (2.0 * math.pi / (4 * freq_count))
    cosine = jnp.cos(angles)
    sine = jnp.sin(angles)
    upper = jnp.concatenate([cosine, sine], axis=1)
    lower = jnp.concatenate([-sine, cosine], axis=1)
    return jnp.stack([upper, lower]).astype(jnp.bfloat16)


def whiten_parts(real_part, imag_part, magnitude, channel_level, usable):
    factor = usable.astype(jnp.float32)[:, None, :] / (magnitude + 0.5 * (channel_level + 1e-05))
    return jnp.stack([real_part * factor, imag_part * factor]).astype(jnp.bfloat16)


def cross_parts(own_real, own_imag, far_real, far_imag):
    own_real = own_real.astype(jnp.float32)
    own_imag = own_imag.astype(jnp.float32)
    far_real = far_real.astype(jnp.float32)
    far_imag = far_imag.astype(jnp.float32)
    return jnp.stack(
        [own_real * far_real + own_imag * far_imag, own_imag * far_real - own_real * far_imag]
    ).astype(jnp.bfloat16)


def pair_terms(corr_all):
    lag_count = corr_all.shape[-1] // 2
    real_corr = corr_all[..., :lag_count]
    imag_corr = corr_all[..., lag_count:]
    power = real_corr * real_corr + imag_corr * imag_corr
    mean_power = jnp.mean(power, axis=-1, keepdims=True)
    denominator = jnp.sqrt(power + 0.25 * (mean_power + 1e-06))
    return (
        jnp.sum(real_corr, axis=-3),
        jnp.sum(real_corr / denominator, axis=-3),
        jnp.sum(imag_corr / denominator, axis=-3),
    )


def whiten_channels(grouped, usable):
    real_part = grouped[0].astype(jnp.float32)
    imag_part = grouped[1].astype(jnp.float32)
    magnitude = jnp.sqrt(real_part * real_part + imag_part * imag_part)
    channel_level = jnp.sum(magnitude, axis=1, keepdims=True) / F
    return jnp.transpose(
        whiten_parts(real_part, imag_part, magnitude, channel_level, usable), (0, 1, 3, 2)
    )


def shards(spectra, quality, offsets):
    chan_count = lax.axis_size("chan")
    tm_count = lax.axis_size("tm")
    levels = chan_count.bit_length() - 1
    table_bf = lag_table(F, LAGS)
    inv_root = 1.0 / math.sqrt(F)
    grouped = lax.all_to_all(spectra, "chan", split_axis=3, concat_axis=2, tiled=True)
    own_quality = lax.dynamic_slice_in_dim(quality, lax.axis_index("chan") * CH_DEV, CH_DEV, 1)
    whitened = whiten_channels(grouped, own_quality)
    moving = jnp.broadcast_to(whitened, (NOFF,) + whitened.shape)
    for bit_index in range(levels):
        step_size = 1 << bit_index
        arrived = shifted(moving, "chan", -step_size)
        chosen = offsets // step_size % 2 == 1
        moving = jnp.where(chosen[:, None, None, None, None], arrived, moving)
    crossed = cross_parts(whitened[0][None], whitened[1][None], moving[:, 0], moving[:, 1])
    corr_all = jnp.einsum("cnwhf,cfl->nwhl", crossed, table_bf, preferred_element_type=jnp.float32)
    linear_sum, real_sum, imag_sum = pair_terms(corr_all * inv_root)
    totals = lax.psum((linear_sum, real_sum, imag_sum), "tm")
    window_count = W_DEV * tm_count
    linear = totals[0] / window_count
    real_phase = totals[1] / window_count
    imag_phase = totals[2] / window_count
    stacks = jnp.transpose(linear * (real_phase * real_phase + imag_phase * imag_phase), (1, 0, 2))
    reverse_part = stacks
    for bit_index in range(levels):
        step_size = 1 << bit_index
        arrived = shifted(reverse_part, "chan", step_size)
        chosen = offsets // step_size % 2 == 1
        reverse_part = jnp.where(chosen[None, :, None], arrived, reverse_part)
    return stacks + jnp.flip(reverse_part, axis=2)


def solution(mesh):
    return jax.shard_map(
        shards,
        mesh=mesh,
        in_specs=(P(None, "tm", "chan", None), P("tm", None), P()),
        out_specs=P("chan", None, None),
        check_vma=False,
    )
```

profile of v0, /device:TPU:1, one launch (start us, length us, event | category | flops | bytes accessed | tf_op | source)
XLA Modules:
  0.0 852.1 jit_solution(3433920633830712305)
XLA Ops:
  6.5 5.9 copy.14
  12.4 7.3 reshape.152
  19.7 12.5 %all-to-all-start = ((bf16[64,2,4096]{2,1,0:T(2,128)(2,1)}), bf16[64,2,4096]{2,1,0:T(2,128)(2,1)S(1)}, u32[]{:S(2)}, u32[]{:S(2)}) async-start(bf16[64,2,4096]{2,1,0:T(2,128)(2,1)} %reshape.152), calls=%async_computation | async-start | bytes 2097152 | tf_op jit(solution)/shard_map/all_to_all | solution.py:78
  32.3 0.8 dynamic-slice_convert_fusion
  33.0 26.5 %all-to-all-done = bf16[64,2,4096]{2,1,0:T(2,128)(2,1)S(1)} async-done(((bf16[64,2,4096]{2,1,0:T(2,128)(2,1)}), bf16[64,2,4096]{2,1,0:T(2,128)(2,1)S(1)}, u32[]{:S(2)}, u32[]{:S(2)}) %all-to-all-start) | async-done | bytes 1048608 | tf_op jit(solution)/shard_map/all_to_all | solution.py:78
  59.5 3.5 reshape.153
  63.0 7.0 copy.16
  70.0 2.4 slice_convert_fusion.1
  72.4 1.0 sqrt_reduce_fusion
  73.4 3.8 copy.17
  77.3 3.8 reshape.144
  81.1 2.8 copy.18
  83.8 3.6 reshape.145
  87.5 0.6 multiply_convert_fusion.1
  88.2 0.5 broadcast_in_dim.92
  88.7 1.5 collective-permute-start
  90.2 89.9 %collective-permute-done = bf16[4,2,8,16,2048]{4,3,2,0,1:T(8,128)(2,1)S(1)} collective-permute-done((bf16[4,2,8,16,2048]{4,3,2,0,1:T(8,128)(2,1)S(1)}, bf16[4,2,8,16,2048]{4,3,2,0,1:T(8,128)(2,1)S(1)}, u32[]{:S(2)}, u32[]{:S(2)}) %collective-permute-start) | collective-permute-done | bytes 4194336 | tf_op jit(solution)/shard_map/ppermute | solution.py:18
  180.2 0.5 broadcast_select_fusion
  180.7 1.3 collective-permute-start.1
  182.0 90.8 %collective-permute-done.1 = bf16[4,2,8,16,2048]{4,3,2,0,1:T(8,128)(2,1)S(1)} collective-permute-done((bf16[4,2,8,16,2048]{4,3,2,0,1:T(8,128)(2,1)S(1)}, bf16[4,2,8,16,2048]{4,3,2,0,1:T(8,128)(2,1)S(1)}, u32[]{:S(2)}, u32[]{:S(2)}) %collective-permute-start.1) | collective-permute-done | bytes 4194336 | tf_op jit(solution)/shard_map/ppermute | solution.py:18
  272.8 0.6 broadcast_select_fusion.1
  273.4 1.3 collective-permute-start.2
  274.7 88.4 %collective-permute-done.2 = bf16[4,2,8,16,2048]{4,3,2,0,1:T(8,128)(2,1)S(1)} collective-permute-done((bf16[4,2,8,16,2048]{4,3,2,0,1:T(8,128)(2,1)S(1)}, bf16[4,2,8,16,2048]{4,3,2,0,1:T(8,128)(2,1)S(1)}, u32[]{:S(2)}, u32[]{:S(2)}) %collective-permute-start.2) | collective-permute-done | bytes 4194336 | tf_op jit(solution)/shard_map/ppermute | solution.py:18
  363.6 1.3 collective-permute-start.3
  364.9 89.1 %collective-permute-done.3 = bf16[4,2,8,16,2048]{4,3,2,0,1:T(8,128)(2,1)S(1)} collective-permute-done((bf16[4,2,8,16,2048]{4,3,2,0,1:T(8,128)(2,1)S(1)}, bf16[4,2,8,16,2048]{4,3,2,0,1:T(8,128)(2,1)S(1)}, u32[]{:S(2)}, u32[]{:S(2)}) %collective-permute-start.3) | collective-permute-done | bytes 4194336 | tf_op jit(solution)/shard_map/ppermute | solution.py:18
  454.5 1.3 collective-permute-start.4
  455.8 90.0 %collective-permute-done.4 = bf16[4,2,8,16,2048]{4,3,2,0,1:T(8,128)(2,1)S(1)} collective-permute-done((bf16[4,2,8,16,2048]{4,3,2,0,1:T(8,128)(2,1)S(1)}, bf16[4,2,8,16,2048]{4,3,2,0,1:T(8,128)(2,1)S(1)}, u32[]{:S(2)}, u32[]{:S(2)}) %collective-permute-start.4) | collective-permute-done | bytes 4194336 | tf_op jit(solution)/shard_map/ppermute | solution.py:18
  546.3 1.3 collective-permute-start.5
  547.6 8.7 %fusion.20 = (bf16[2048,256]{1,0:T(8,128)(2,1)S(1)}, bf16[2048,256]{1,0:T(8,128)(2,1)S(1)}, bf16[2048,256]{1,0:T(8,128)(2,1)S(1)}) fusion(s32[256]{0:T(256)S(1)} %multiply_add_fusion.1), kind=kLoop, calls=%fused_computation.42 | loop fusion | flops 9437184 | bytes 3146752 | tf_op jit(solution)/shard_map/convert.13
  556.9 174.4 %collective-permute-done.5 = bf16[4,2,8,16,2048]{4,3,2,0,1:T(8,128)(2,1)S(1)} collective-permute-done((bf16[4,2,8,16,2048]{4,3,2,0,1:T(8,128)(2,1)S(1)}, bf16[4,2,8,16,2048]{4,3,2,0,1:T(8,128)(2,1)S(1)}, u32[]{:S(2)}, u32[]{:S(2)}) %collective-permute-start.5) | collective-permute-done | bytes 4194336 | tf_op jit(solution)/shard_map/ppermute | solution.py:18
  731.8 1.4 fusion.1
  733.3 2.3 fusion.21
  735.8 1.0 divide_reduce_fusion.1
  736.8 63.1 %all-reduce.3.cloned.1.call-done = (f32[4,16,256]{2,1,0:T(8,128)}, f32[4,16,256]{2,1,0:T(8,128)}, f32[4,16,256]{2,1,0:T(8,128)}) async-done(((f32[4,16,256]{2,1,0:T(8,128)}, f32[4,16,256]{2,1,0:T(8,128)}, f32[4,16,256]{2,1,0:T(8,128)}), (f32[4,16,256]{2,1,0:T(8,128)}, f32[4,16,256]{2,1,0:T(8,128)}, f32[4,16,256]{2,1,0:T(8,128)})) %all-reduce.3.cloned.1.call-update) | async-done | bytes 196624 | tf_op jit(solution)/shard_map/psum | solution.py:90
  799.9 0.9 multiply_bitcast_fusion
  800.8 3.1 collective-permute-start.6
  803.9 1.3 collective-permute-done.6
  805.3 5.6 collective-permute-start.7
  810.9 1.3 collective-permute-done.7
  812.3 6.7 collective-permute-start.8
  819.0 1.3 collective-permute-done.8
  820.4 5.2 collective-permute-start.9
  825.6 1.3 collective-permute-done.9
  827.0 10.0 %collective-permute-start.10 = (f32[16,4,256]{2,0,1:T(8,128)S(1)}, f32[16,4,256]{2,0,1:T(8,128)S(1)}, u32[]{:S(2)}, u32[]{:S(2)}) collective-permute-start(f32[16,4,256]{2,0,1:T(8,128)S(1)} %broadcast_select_fusion.9), channel_id=1, source_target_pairs={{0,64},{4,68},{8,72},{12,76},{16,80},{20,84},{24,88},{28,92},{32,9... | collective-permute-start | bytes 196616 | tf_op jit(solution)/shard_map/ppermute | solution.py:18
  837.0 1.3 collective-permute-done.10
  838.4 4.0 collective-permute-start.11
  842.4 1.8 collective-permute-done.11
  844.5 0.7 copy.19
  (26 shorter events, 3.5 us)
Async XLA Ops:
  19.7 39.8 %all-to-all-start = ((bf16[64,2,4096]{2,1,0:T(2,128)(2,1)}), bf16[64,2,4096]{2,1,0:T(2,128)(2,1)S(1)}, u32[]{:S(2)}, u32[]{:S(2)}) async-start(bf16[64,2,4096]{2,1,0:T(2,128)(2,1)} %reshape.152), calls=%async_computation | async-start | bytes 2097152 | tf_op jit(solution)/shard_map/all_to_all | solution.py:78
  32.2 767.7 %all-reduce.3.cloned.1.call-start = ((), (), s32[]{:S(2)}) async-start(), calls=%async_computation.1 | async-start | bytes 393216 | tf_op jit(solution)/shard_map/psum | solution.py:90
  77.3 3.8 copy-start
  88.1 2.1 copy-start.1
  88.7 91.4 %collective-permute-start = (bf16[4,2,8,16,2048]{4,3,2,0,1:T(8,128)(2,1)S(1)}, bf16[4,2,8,16,2048]{4,3,2,0,1:T(8,128)(2,1)S(1)}, u32[]{:S(2)}, u32[]{:S(2)}) collective-permute-start(bf16[4,2,8,16,2048]{4,3,2,0,1:T(8,128)(2,1)S(1)} %broadcast_in_dim.92), channel_id=1, source_target_pairs={{4,0},{8,4},{12,8},{16,12},{20,16},{24,20},{28,24},{32,28},{36,32}... | collective-permute-start | bytes 12582920 | tf_op jit(solution)/shard_map/ppermute | solution.py:18
  180.7 92.1 %collective-permute-start.1 = (bf16[4,2,8,16,2048]{4,3,2,0,1:T(8,128)(2,1)S(1)}, bf16[4,2,8,16,2048]{4,3,2,0,1:T(8,128)(2,1)S(1)}, u32[]{:S(2)}, u32[]{:S(2)}) collective-permute-start(bf16[4,2,8,16,2048]{4,3,2,0,1:T(8,128)(2,1)S(1)} %broadcast_select_fusion), channel_id=1, source_target_pairs={{8,0},{12,4},{16,8},{20,12},{24,16},{28,20},{32,24},{36,28},{40,32... | collective-permute-start | bytes 12582920 | tf_op jit(solution)/shard_map/ppermute | solution.py:18
  273.4 89.7 %collective-permute-start.2 = (bf16[4,2,8,16,2048]{4,3,2,0,1:T(8,128)(2,1)S(1)}, bf16[4,2,8,16,2048]{4,3,2,0,1:T(8,128)(2,1)S(1)}, u32[]{:S(2)}, u32[]{:S(2)}) collective-permute-start(bf16[4,2,8,16,2048]{4,3,2,0,1:T(8,128)(2,1)S(1)} %broadcast_select_fusion.1), channel_id=1, source_target_pairs={{16,0},{20,4},{24,8},{28,12},{32,16},{36,20},{40,24},{44,28},{48,3... | collective-permute-start | bytes 12582920 | tf_op jit(solution)/shard_map/ppermute | solution.py:18
  363.6 90.4 %collective-permute-start.3 = (bf16[4,2,8,16,2048]{4,3,2,0,1:T(8,128)(2,1)S(1)}, bf16[4,2,8,16,2048]{4,3,2,0,1:T(8,128)(2,1)S(1)}, u32[]{:S(2)}, u32[]{:S(2)}) collective-permute-start(bf16[4,2,8,16,2048]{4,3,2,0,1:T(8,128)(2,1)S(1)} %broadcast_select_fusion.2), channel_id=1, source_target_pairs={{32,0},{36,4},{40,8},{44,12},{48,16},{52,20},{56,24},{60,28},{64,3... | collective-permute-start | bytes 12582920 | tf_op jit(solution)/shard_map/ppermute | solution.py:18
  454.5 91.3 %collective-permute-start.4 = (bf16[4,2,8,16,2048]{4,3,2,0,1:T(8,128)(2,1)S(1)}, bf16[4,2,8,16,2048]{4,3,2,0,1:T(8,128)(2,1)S(1)}, u32[]{:S(2)}, u32[]{:S(2)}) collective-permute-start(bf16[4,2,8,16,2048]{4,3,2,0,1:T(8,128)(2,1)S(1)} %broadcast_select_fusion.3), channel_id=1, source_target_pairs={{64,0},{68,4},{72,8},{76,12},{80,16},{84,20},{88,24},{92,28},{96,3... | collective-permute-start | bytes 12582920 | tf_op jit(solution)/shard_map/ppermute | solution.py:18
  546.3 185.0 %collective-permute-start.5 = (bf16[4,2,8,16,2048]{4,3,2,0,1:T(8,128)(2,1)S(1)}, bf16[4,2,8,16,2048]{4,3,2,0,1:T(8,128)(2,1)S(1)}, u32[]{:S(2)}, u32[]{:S(2)}) collective-permute-start(bf16[4,2,8,16,2048]{4,3,2,0,1:T(8,128)(2,1)S(1)} %broadcast_select_fusion.4), channel_id=1, source_target_pairs={{128,0},{132,4},{136,8},{140,12},{144,16},{148,20},{152,24},{156,2... | collective-permute-start | bytes 12582920 | tf_op jit(solution)/shard_map/ppermute | solution.py:18
  800.8 4.4 collective-permute-start.6
  805.3 6.9 collective-permute-start.7
  812.3 8.0 collective-permute-start.8
  820.4 6.5 collective-permute-start.9
  827.0 11.3 %collective-permute-start.10 = (f32[16,4,256]{2,0,1:T(8,128)S(1)}, f32[16,4,256]{2,0,1:T(8,128)S(1)}, u32[]{:S(2)}, u32[]{:S(2)}) collective-permute-start(f32[16,4,256]{2,0,1:T(8,128)S(1)} %broadcast_select_fusion.9), channel_id=1, source_target_pairs={{0,64},{4,68},{8,72},{12,76},{16,80},{20,84},{24,88},{28,92},{32,9... | collective-permute-start | bytes 196616 | tf_op jit(solution)/shard_map/ppermute | solution.py:18
  838.4 5.9 collective-permute-start.11
Sparse Core Ops, SparseCore 0:
  736.9 62.9 all-reduce.2
where the time goes:
time: 858 us; the launch traced here: 852 us
  waiting for transfers between devices  721 us (84%)
  starting transfers between devices  55.1 us (6%)
  local copies, waits for them, and re-layouts  38.9 us (5%)
  other arithmetic  21.3 us (2%)
  between operations  13.7 us (2%)
    ppermute x12, waiting for transfers between devices, shifted(): lax.ppermute(value, axis, [(source, source + steps) for source in range(l...  631 us
    psum x1, waiting for transfers between devices, shards(): totals = lax.psum((linear_sum, real_sum, imag_sum), 'tm')  63.1 us
    ppermute x12, starting transfers between devices, shifted(): lax.ppermute(value, axis, [(source, source + steps) for source in range(l...  42.6 us
    all_to_all x1, waiting for transfers between devices, shards(): lax.all_to_all(spectra, 'chan', split_axis=3, concat_axis=2, tiled=True)  26.5 us
  transfers between devices with their start and end apart: 14, of which 14 were waited for; matrix products, arithmetic and copies ran while one was open for 1% of the time, Pallas kernels for 0%

commit v1 on v0

v1 whole, which is shorter than its diff:
```python
import math

import jax
import jax.numpy as jnp
import numpy as np
from jax import lax
from jax.experimental import pallas as pl
from jax.experimental.pallas import tpu as pltpu
from jax.sharding import PartitionSpec as P

MESH = pl.DeviceIdType.MESH
F = 2048
LAGS = 256
HALF = 128
NOFF = 4
WINDOWS = 32
NCH = 1024
TILE = 128
NEED = 5
FB = 32
BF = jnp.bfloat16
F32 = jnp.float32


def place():
    chan = lax.axis_index("chan")
    tm = lax.axis_index("tm")
    return chan // 16, (chan // 4) % 4, chan % 4, tm // 2, tm % 2


def half_table():
    freq = np.arange(F, dtype=np.int64)[None, :]
    lag = 2 * np.arange(HALF, dtype=np.int64)[:, None] + 1
    angle = ((freq * lag) % (4 * F)).astype(np.float64) * (2.0 * math.pi / (4 * F))
    return np.concatenate([np.cos(angle), np.sin(angle)]).astype(np.float32)


def gather_kernel(spec_ref, qual_ref, g_ref, q_ref, send_sem, recv_sem, qsem):
    z, y, x, zh, core = place()
    chan = z * 16 + y * 4 + x
    sib = zh * 2 + 1 - core
    tm = zh * 2 + core
    par = (core + x + 1 + x // 2) % 2
    up = z * 16 + ((y + 1) % 4) * 4 + x
    down = z * 16 + ((y + 3) % 4) * 4 + x

    barrier = pltpu.get_barrier_semaphore()
    spots = [(dz, xh) for dz in (0, 1, 3, 2) for xh in (0, 1)]

    def source(spot):
        return (z + spot[0]) % 4 * 16 + 2 * spot[1] + par

    for spot in spots:
        pl.semaphore_signal(
            barrier, inc=1, device_id=(source(spot) + y * 4, zh * 2 + x // 2), device_id_type=MESH
        )
    for there in ((up, tm), (down, tm), (chan, sib)):
        pl.semaphore_signal(barrier, inc=1, device_id=there, device_id_type=MESH)
    pl.semaphore_wait(barrier, 11)

    started = []

    def forward(block, there):
        copy = pltpu.make_async_remote_copy(
            src_ref=g_ref.at[block],
            dst_ref=g_ref.at[block],
            send_sem=send_sem.at[len(started)],
            recv_sem=recv_sem.at[block],
            device_id=there,
            device_id_type=MESH,
        )
        copy.start()
        started.append(copy)

    def arrive(block):
        pltpu.make_async_remote_copy(
            src_ref=g_ref.at[block],
            dst_ref=g_ref.at[block],
            send_sem=send_sem.at[0],
            recv_sem=recv_sem.at[block],
            device_id=(chan, sib),
            device_id_type=MESH,
        ).wait_recv()

    for dz, low in spots:
        zt = (z + dz) % 4
        copy = pltpu.make_async_remote_copy(
            src_ref=spec_ref.at[:, 2 * zt + low],
            dst_ref=g_ref.at[chan],
            send_sem=send_sem.at[len(started)],
            recv_sem=recv_sem.at[chan],
            device_id=(zt * 16 + y * 4 + low + 2 * core, zh * 2 + (x + low + 1 + core) % 2),
            device_id_type=MESH,
        )
        copy.start()
        started.append(copy)
    qcopy = pltpu.make_async_remote_copy(
        src_ref=qual_ref,
        dst_ref=q_ref,
        send_sem=qsem.at[0],
        recv_sem=qsem.at[1],
        device_id=(chan, sib),
        device_id_type=MESH,
    )
    qcopy.start()

    def own(n):
        block = source(spots[n]) + y * 4
        arrive(block)
        forward(block, (up, tm))
        forward(block, (down, tm))
        forward(block, (chan, sib))

    def near(n):
        block = source(spots[n]) + (y + 3) % 4 * 4
        arrive(block)
        if n < 4:
            forward(block, (up, tm))
        forward(block, (chan, sib))
        block = source(spots[n]) + (y + 1) % 4 * 4
        arrive(block)
        if n >= 4:
            forward(block, (down, tm))
        forward(block, (chan, sib))

    def far(n):
        block = source(spots[n]) + (y + 2) % 4 * 4
        arrive(block)
        forward(block, (chan, sib))

    for n in range(10):
        if n < 8:
            own(n)
        if 0 <= n - 1 < 8:
            near(n - 1)
        if 0 <= n - 2 < 8:
            far(n - 2)
    for n in range(8):
        for dy in range(4):
            zs = (z + spots[n][0]) % 4
            arrive(zs * 16 + (y + dy) % 4 * 4 + 2 * spots[n][1] + 1 - par)
    qcopy.wait()
    for copy in started:
        copy.wait_send()


def gather_window(spectra, quality):
    any_spec = pl.BlockSpec(memory_space=pl.ANY)
    return pl.pallas_call(
        gather_kernel,
        name="gather_window",
        out_shape=(
            jax.ShapeDtypeStruct((64, 2, FB, NCH), BF),
            jax.ShapeDtypeStruct((8, NCH), jnp.int32),
        ),
        in_specs=[any_spec, any_spec],
        out_specs=(any_spec, any_spec),
        scratch_shapes=[
            pltpu.SemaphoreType.DMA((64,)),
            pltpu.SemaphoreType.DMA((64,)),
            pltpu.SemaphoreType.DMA((2,)),
        ],
        compiler_params=pltpu.CompilerParams(collective_id=0, has_side_effects=True),
    )(spectra, quality)


def corr_kernel(sc_ref, g_ref, qual_ref, tab_ref, out_ref, w_ref, mag_ref, acc_ref, x_ref):
    step = pl.program_id(0)

    @pl.when(step < NEED)
    def _():
        def measure(n, total):
            re = g_ref[n, 0].astype(F32)
            im = g_ref[n, 1].astype(F32)
            mag = jnp.sqrt(re * re + im * im)
            mag_ref[n] = mag
            return total + mag

        total = lax.fori_loop(0, 64, measure, jnp.zeros((FB, TILE), F32), unroll=4)
        level = jnp.sum(total, axis=0, keepdims=True) / F
        add = 0.5 * (level + 1e-05)
        live = jnp.where(sc_ref[0] + step < 8, 1.0, 0.0).astype(F32)
        usable = qual_ref[0:1, :].astype(F32) * live

        def whiten(n, carry):
            factor = usable / (mag_ref[n] + add)
            w_ref[step, 0, n] = (g_ref[n, 0].astype(F32) * factor).astype(BF)
            w_ref[step, 1, n] = (g_ref[n, 1].astype(F32) * factor).astype(BF)
            return carry

        lax.fori_loop(0, 64, whiten, 0, unroll=4)

    @pl.when(step == NEED)
    def _():
        lane = lax.broadcasted_iota(jnp.int32, (256, TILE), 1)
        for n in range(8):
            rows = pl.ds(8 * n, 8)

            def grab(tile, part, rows=rows):
                return w_ref[tile, part, rows].astype(F32).reshape(256, TILE)

            own_re = grab(0, 0)
            own_im = grab(0, 1)
            for j in range(NOFF):
                whole = sc_ref[1 + j] // 8
                rest = sc_ref[1 + j] % 8 * 16
                keep = lane >= rest
                back = (TILE - rest) % TILE
                far_re = pltpu.roll(jnp.where(keep, grab(whole, 0), grab(whole + 1, 0)), back, 1)
                far_im = pltpu.roll(jnp.where(keep, grab(whole, 1), grab(whole + 1, 1)), back, 1)
                x_ref[:, j * TILE : (j + 1) * TILE] = (own_re * far_re + own_im * far_im).astype(BF)
                x_ref[:, 512 + j * TILE : 512 + (j + 1) * TILE] = (own_im * far_re - own_re * far_im).astype(BF)
            part = jnp.dot(tab_ref[:, 256 * n : 256 * (n + 1)], x_ref[...], preferred_element_type=F32)
            if n == 0:
                acc_ref[...] = part
            else:
                acc_ref[...] += part
        scale = 1.0 / math.sqrt(F)
        for j in range(NOFF):
            left = slice(j * TILE, (j + 1) * TILE)
            right = slice(512 + j * TILE, 512 + (j + 1) * TILE)
            a = acc_ref[:HALF, left]
            b = acc_ref[HALF:, right]
            c = acc_ref[HALF:, left]
            d = acc_ref[:HALF, right]
            pos_r = (a - b) * scale
            neg_r = (a + b) * scale
            pos_q = (d + c) * scale
            neg_q = (d - c) * scale
            pos_p = pos_r * pos_r + pos_q * pos_q
            neg_p = neg_r * neg_r + neg_q * neg_q
            mean = jnp.sum(pos_p + neg_p, axis=0, keepdims=True) / LAGS
            floor = 0.25 * (mean + 1e-06)
            pos_d = jnp.sqrt(pos_p + floor)
            neg_d = jnp.sqrt(neg_p + floor)
            out_ref[0, 0, :, left] = pos_r
            out_ref[0, 1, :, left] = neg_r
            out_ref[1, 0, :, left] = pos_r / pos_d
            out_ref[1, 1, :, left] = neg_r / neg_d
            out_ref[2, 0, :, left] = pos_q / pos_d
            out_ref[2, 1, :, left] = neg_q / neg_d


def correlate(scalars, gathered, usable, table):
    grid_spec = pltpu.PrefetchScalarGridSpec(
        num_scalar_prefetch=1,
        grid=(NEED + 1,),
        in_specs=[
            pl.BlockSpec((64, 2, FB, TILE), lambda s, sc: (0, 0, 0, jnp.minimum(sc[0] + jnp.minimum(s, NEED - 1), 7))),
            pl.BlockSpec((8, TILE), lambda s, sc: (0, jnp.minimum(sc[0] + jnp.minimum(s, NEED - 1), 7))),
            pl.BlockSpec((2 * HALF, F), lambda s, sc: (0, 0)),
        ],
        out_specs=pl.BlockSpec((3, 2, HALF, NOFF * TILE), lambda s, sc: (0, 0, 0, 0)),
        scratch_shapes=[
            pltpu.VMEM((NEED + 1, 2, 64, FB, TILE), BF),
            pltpu.VMEM((64, FB, TILE), F32),
            pltpu.VMEM((2 * HALF, 2 * NOFF * TILE), F32),
            pltpu.VMEM((256, 2 * NOFF * TILE), BF),
        ],
    )
    return pl.pallas_call(
        corr_kernel,
        name="correlate",
        grid_spec=grid_spec,
        out_shape=jax.ShapeDtypeStruct((3, 2, HALF, NOFF * TILE), F32),
    )(scalars, gathered, usable, table)


def tail_kernel(off_ref, p_ref, out_ref, xbuf, zacc, zbuf, st, tbuf, jbuf, mbuf, rbuf, send_sem, recv_sem):
    zl, y, x, zh, core = place()
    chan = zl * 16 + y * 4 + x
    tm = zh * 2 + core
    z = zh * 4 + zl
    t = y * 2 + core

    def x_peer(d):
        return (zl * 16 + y * 4 + (x + d) % 4, tm)

    def z_peer(d):
        there = (z + d) % 8
        return (there % 4 * 16 + y * 4 + x, there // 4 * 2 + core)

    def t_peer(d):
        there = (t + d) % 8
        return (zl * 16 + there // 2 * 4 + x, zh * 2 + there % 2)

    barrier = pltpu.get_barrier_semaphore()
    peers = [x_peer(d) for d in (1, 2, 3)] + [z_peer(d) for d in range(1, 8)] + [t_peer(d) for d in range(1, 8)]
    for there in peers:
        pl.semaphore_signal(barrier, inc=1, device_id=there, device_id_type=MESH)
    pl.semaphore_wait(barrier, len(peers))

    started = []

    def send(src, dst, there):
        copy = pltpu.make_async_remote_copy(
            src_ref=src,
            dst_ref=dst,
            send_sem=send_sem.at[len(started)],
            recv_sem=recv_sem.at[len(started)],
            device_id=there,
            device_id_type=MESH,
        )
        copy.start()
        started.append(copy)
        return copy

    def columns(where):
        return pl.ds(pl.multiple_of(where * TILE, TILE), TILE)

    copies = [
        send(p_ref.at[:, :, :, columns((x + d) % 4)], xbuf.at[d - 1], x_peer(d)) for d in (1, 2, 3)
    ]
    for copy in copies:
        copy.wait_recv()
    mine = p_ref[:, :, :, columns(x)]
    zacc[...] = (mine + xbuf[0]) + (xbuf[1] + xbuf[2])

    def lag_rows(where):
        return pl.ds(pl.multiple_of(where * 16, 16), 16)

    copies = [
        send(zacc.at[:, :, lag_rows((z + d) % 8)], zbuf.at[d - 1], z_peer(d)) for d in range(1, 8)
    ]
    total = zacc[:, :, lag_rows(z)]
    for d, copy in enumerate(copies):
        copy.wait_recv()
        total = total + zbuf[d]
    linear = total[0] / WINDOWS
    real = total[1] / WINDOWS
    imag = total[2] / WINDOWS
    st[t] = linear * (real * real + imag * imag)

    copies = [send(st.at[t], st.at[t], t_peer(d)) for d in range(1, 8)]
    for copy in copies:
        copy.wait_recv()
    shift = off_ref[x]
    whole = shift // 8
    rest = shift % 8 * 16
    lane = lax.broadcasted_iota(jnp.int32, (2, 16, TILE), 2)
    pieces = []
    for n in range(4):
        tile = 2 * n + y // 2
        first = tile - whole
        a = jnp.where(first >= 0, st[jnp.maximum(first, 0)], 0.0)
        b = jnp.where(first >= 1, st[jnp.maximum(first - 1, 0)], 0.0)
        rev = pltpu.roll(jnp.where(lane < TILE - rest, a, b).reshape(32, TILE), rest, 1).reshape(2, 16, TILE)
        ahead = st[tile]
        pieces.append(ahead[0] + rev[1])
        pieces.append(ahead[1] + rev[0])
    tbuf[...] = jnp.concatenate(pieces, axis=0).T

    def channel_rows(where):
        return pl.ds(pl.multiple_of(y % 2 * 64 + where * 16, 16), 16)

    copies = [send(tbuf.at[channel_rows((x + d) % 4)], jbuf.at[x], x_peer(d)) for d in (1, 2, 3)]
    jbuf[x] = tbuf[channel_rows(x)]
    for copy in copies:
        copy.wait_recv()
    group = lax.broadcasted_iota(jnp.int32, (16, TILE), 1) // 32
    for n in range(4):
        merged = jnp.zeros((16, TILE), F32)
        for j in range(NOFF):
            merged = jnp.where(group == j, pltpu.roll(jbuf[j], (32 * (j - n)) % TILE, 1), merged)
        mbuf[n] = merged
    copies = [send(mbuf.at[(z + d) % 4], rbuf.at[z], z_peer(d)) for d in range(1, 8)]
    rbuf[z] = mbuf[z % 4]
    for copy in copies:
        copy.wait_recv()
    span = lax.broadcasted_iota(jnp.int32, (16, TILE), 1) // 16
    for j in range(NOFF):
        for s in range(2):
            merged = jnp.zeros((16, TILE), F32)
            for n in range(8):
                merged = jnp.where(span == n, pltpu.roll(rbuf[n], (16 * n - 32 * j - 16 * s) % TILE, 1), merged)
            out_ref[j, s] = merged
    for copy in started:
        copy.wait_send()


def finish(offsets, sums):
    count = 3 + 7 + 7 + 3 + 7
    vmem = pl.BlockSpec(memory_space=pltpu.VMEM)
    return pl.pallas_call(
        tail_kernel,
        name="finish",
        out_shape=jax.ShapeDtypeStruct((NOFF, 2, 16, TILE), F32),
        in_specs=[pl.BlockSpec(memory_space=pltpu.SMEM), vmem],
        out_specs=vmem,
        scratch_shapes=[
            pltpu.VMEM((3, 3, 2, HALF, TILE), F32),
            pltpu.VMEM((3, 2, HALF, TILE), F32),
            pltpu.VMEM((7, 3, 2, 16, TILE), F32),
            pltpu.VMEM((8, 2, 16, TILE), F32),
            pltpu.VMEM((TILE, TILE), F32),
            pltpu.VMEM((NOFF, 16, TILE), F32),
            pltpu.VMEM((4, 16, TILE), F32),
            pltpu.VMEM((8, 16, TILE), F32),
            pltpu.SemaphoreType.DMA((count,)),
            pltpu.SemaphoreType.DMA((count,)),
        ],
        compiler_params=pltpu.CompilerParams(collective_id=1, has_side_effects=True),
    )(offsets, sums)


def shards(spectra, quality, offsets):
    z, y, x, zh, core = place()
    gathered, other = gather_window(spectra, quality)
    mine = jnp.where(x // 2 == core, quality, other)
    usable = lax.dynamic_slice_in_dim(mine, 2 * z + x % 2, 1, 0)
    usable = jnp.broadcast_to(usable, (8, NCH))
    table = jnp.asarray(half_table()).astype(BF)
    scalars = jnp.concatenate([(y * 2 + core).astype(jnp.int32)[None], offsets.astype(jnp.int32)])
    sums = correlate(scalars, gathered, usable, table)
    halves = finish(offsets, sums)
    late = jnp.transpose(halves[:, 0], (1, 0, 2))
    early = jnp.flip(jnp.transpose(halves[:, 1], (1, 0, 2)), axis=2)
    return jnp.concatenate([early, late], axis=2)


def solution(mesh):
    return jax.shard_map(
        shards,
        mesh=mesh,
        in_specs=(P(None, "tm", "chan", None), P("tm", None), P()),
        out_specs=P("chan", None, None),
        check_vma=False,
    )
```

time: 858 us -> 131 us (0.15)
  waiting for transfers between devices: 721 us -> 0 us
  Pallas kernels: 0 us -> 125 us
  starting transfers between devices: 55.1 us -> 0 us
  local copies, waits for them, and re-layouts: 38.9 us -> 2.15 us
  other arithmetic: 21.3 us -> 2.12 us
  between operations: 13.7 us -> 0.02 us
    ppermute x12 -> x0, waiting for transfers between devices: 631 us -> none  [shifted(): lax.ppermute(value, axis, [(source, source + steps) for source in range(l...]
    pallas_call x0 -> x3, Pallas kernels: none -> 125 us  [the longest x1 63.3 us: gather_window(): pl.pallas_call(gather_kernel, name='gather_window', out_shape=(jax.ShapeD...]
    psum x1 -> x0, waiting for transfers between devices: 63.1 us -> none  [shards(): totals = lax.psum((linear_sum, real_sum, imag_sum), 'tm')]
    ppermute x12 -> x0, starting transfers between devices: 42.6 us -> none  [shifted(): lax.ppermute(value, axis, [(source, source + steps) for source in range(l...]
    all_to_all x1 -> x0, waiting for transfers between devices: 26.5 us -> none  [shards(): lax.all_to_all(spectra, 'chan', split_axis=3, concat_axis=2, tiled=True)]
    unnamed x7 -> x0, local copies, waits for them, and re-layouts: 16.6 us -> none
    convert_element_type x4 -> x0, local copies, waits for them, and re-layouts: 14 us -> none  [the longest x2 7.63 us: whiten_channels(): real_part = grouped[0].astype(jnp.float32)]
    all_to_all x1 -> x0, starting transfers between devices: 12.5 us -> none  [shards(): lax.all_to_all(spectra, 'chan', split_axis=3, concat_axis=2, tiled=True)]
  transfers between devices with their start and end apart: 14 -> 0, of which waited for: 14 -> 0; matrix products, arithmetic and copies ran while one was open for 1% -> 0% of each run, Pallas kernels for 0% -> 0%
where the time goes in v1:
time: 131 us; the launch traced here: 129 us
  Pallas kernels  125 us (95%)
  local copies, waits for them, and re-layouts  2.15 us (2%)
  other arithmetic  2.12 us (2%)
    pallas_call x1, Pallas kernels, gather_window(): pl.pallas_call(gather_kernel, name='gather_window', out_shape=(jax.ShapeD...  63.3 us
    pallas_call x1, Pallas kernels, finish(): pl.pallas_call(tail_kernel, name='finish', out_shape=jax.ShapeDtypeStruct...  49.3 us
    pallas_call x1, Pallas kernels, correlate(): pl.pallas_call(corr_kernel, name='correlate', grid_spec=grid_spec, out_sh...  12.1 us

profile of v1, /device:TPU:1, one launch (start us, length us, event | category | flops | bytes accessed | tf_op | source)
XLA Modules:
  0.0 129.1 jit_solution(10473840254916310246)
XLA Ops:
  0.0 1.3 %pad_add_fusion.sc_ref = s32[5]{0:T(128)} fusion(s32[4]{0:T(128)} %off_ref.1, s32[1]{0:T(128)} %bitcast), kind=kLoop, calls=%fused_computation.4 | loop fusion | flops 5 | bytes 40 | tf_op jit(solution)/shard_map/concatenate | solution.py:413
  1.3 63.3 %gather_window.1 = (bf16[64,2,32,1024]{3,2,1,0:T(8,128)(2,1)}, s32[8,1024]{1,0:T(8,128)}) custom-call(bf16[2,8,32,1024]{3,2,1,0:T(8,128)(2,1)} %spec_ref.1, s32[8,1024]{1,0:T(8,128)} %qual_ref.1), custom_call_target="tpu_custom_call" | custom-call | tf_op jit(solution)/shard_map/gather_window/pallas_call | solution.py:149
  64.7 0.8 broadcast_select_fusion
  65.5 0.6 broadcast_in_dim.12.qual_ref
  66.1 12.1 %correlate.1.p_ref = f32[3,2,128,512]{3,2,1,0:T(8,128)} custom-call(s32[5]{0:T(128)} %pad_add_fusion.sc_ref, bf16[64,2,32,1024]{3,2,1,0:T(8,128)(2,1)} %get-tuple-element.7.g_ref, s32[8,1024]{1,0:T(8,128)} %broadcast_in_dim.12.qual_ref, bf16[256,2048]{1,0:T(8,128)(2,1)} %constant.76.tab_ref), custom_call_target="tpu_custom_call" | custom-call | tf_op jit(solution)/shard_map/correlate/pallas_call | solution.py:261
  78.2 49.3 %finish.1 = f32[4,2,16,128]{3,2,1,0:T(8,128)} custom-call(s32[4]{0:T(128)} %off_ref.1, f32[3,2,128,512]{3,2,1,0:T(8,128)} %correlate.1.p_ref), custom_call_target="tpu_custom_call" | custom-call | tf_op jit(solution)/shard_map/finish/pallas_call | solution.py:384
  127.6 0.8 slice_bitcast_fusion.1
  128.3 0.1 rev.4
  128.4 0.7 copy.6
  (1 shorter events, 0.0 us)

commit v2 on v0

v2 whole, which is shorter than its diff:
```python
import math

import jax
import jax.numpy as jnp
import numpy as np
from jax import lax
from jax.experimental import pallas as pl
from jax.experimental.pallas import tpu as pltpu
from jax.sharding import PartitionSpec as P

MESH = pl.DeviceIdType.MESH
F = 2048
LAGS = 256
HALF = 128
NOFF = 4
WINDOWS = 32
NCH = 1024
TILE = 128
NEED = 5
FB = 32
GROUP = 256
BF = jnp.bfloat16
F32 = jnp.float32


def place():
    chan = lax.axis_index("chan")
    tm = lax.axis_index("tm")
    return chan // 16, (chan // 4) % 4, chan % 4, tm // 2, tm % 2


def half_table():
    y, par, z, half, low = np.meshgrid(*(np.arange(n) for n in (4, 2, 4, 2, FB)), indexing="ij")
    freq = ((z * 16 + y * 4 + 2 * half + par) * FB + low).reshape(8, 1, GROUP).astype(np.int64)
    lag = (2 * np.arange(HALF, dtype=np.int64) + 1)[None, :, None]
    angle = ((freq * lag) % (4 * F)).astype(np.float64) * (2.0 * math.pi / (4 * F))
    return np.concatenate([np.cos(angle), np.sin(angle)], axis=1).astype(np.float32)


def tile_at(where):
    return pl.ds(pl.multiple_of(where * TILE, TILE), TILE)


def window_kernel(
    off_ref, spec_ref, qual_ref, tab_ref, out_ref,
    g, qbuf, lvall, add_ref, use_ref, w, xmat, acc, p,
    ring, ringsum, ringin, zacc, zbuf, st, tbuf, jbuf, mbuf, rbuf,
    gsend, grecv, send_sem, recv_sem,
):
    z, y, x, zh, core = place()
    chan = z * 16 + y * 4 + x
    tm = zh * 2 + core
    sib = (chan, zh * 2 + 1 - core)
    t = y * 2 + core
    zall = zh * 4 + z
    par = (core + x + 1 + x // 2) % 2
    up = (z * 16 + ((y + 1) % 4) * 4 + x, tm)
    down = (z * 16 + ((y + 3) % 4) * 4 + x, tm)

    def x_peer(d):
        return (z * 16 + y * 4 + (x + d) % 4, tm)

    def z_peer(d):
        there = (zall + d) % 8
        return (there % 4 * 16 + y * 4 + x, there // 4 * 2 + core)

    def t_peer(d):
        there = (t + d) % 8
        return (z * 16 + there // 2 * 4 + x, zh * 2 + there % 2)

    mate = z + 1 - 2 * (z % 2)
    zs = [z, mate, 3 - z, 3 - mate]
    spots = [(zs[k], xh) for k in range(4) for xh in (0, 1)]

    barrier = pltpu.get_barrier_semaphore()
    greet = [(zt * 16 + y * 4 + 2 * xh + par, zh * 2 + x // 2) for zt, xh in spots]
    greet += [x_peer(d) for d in (1, 2, 3)]
    greet += [z_peer(d) for d in range(1, 8)]
    greet += [t_peer(d) for d in range(1, 8)]
    for there in greet:
        pl.semaphore_signal(barrier, inc=1, device_id=there, device_id_type=MESH)
    pl.semaphore_wait(barrier, len(greet))

    sent = []
    started = []

    def put(src, where, there):
        copy = pltpu.make_async_remote_copy(
            src_ref=src,
            dst_ref=g.at[where[0], where[1]],
            send_sem=gsend.at[len(sent)],
            recv_sem=grecv.at[where[0], where[1]],
            device_id=there,
            device_id_type=MESH,
        )
        copy.start()
        sent.append(len(sent))

    def forward(where, there):
        put(g.at[where[0], where[1]], where, there)

    def arrive(where):
        pltpu.make_async_remote_copy(
            src_ref=g.at[where[0], where[1]],
            dst_ref=g.at[where[0], where[1]],
            send_sem=gsend.at[0],
            recv_sem=grecv.at[where[0], where[1]],
            device_id=sib,
            device_id_type=MESH,
        ).wait_recv()

    def send(src, dst, there):
        copy = pltpu.make_async_remote_copy(
            src_ref=src,
            dst_ref=dst,
            send_sem=send_sem.at[len(started)],
            recv_sem=recv_sem.at[len(started)],
            device_id=there,
            device_id_type=MESH,
        )
        copy.start()
        started.append(copy)
        return copy

    home = (y * 2 + x % 2, z * 2 + x // 2)
    for zt, low in spots:
        put(
            spec_ref.at[:, 2 * zt + low],
            home,
            (zt * 16 + y * 4 + low + 2 * core, zh * 2 + (x + low + 1 + core) % 2),
        )
    qcopy = send(qual_ref, qbuf, sib)

    def block(n, dy):
        return ((y + dy) % 4 * 2 + par, spots[n][0] * 2 + spots[n][1])

    def own(n):
        here = block(n, 0)
        arrive(here)
        forward(here, up)
        forward(here, down)
        forward(here, sib)
        re = g[here[0], here[1], 0].astype(F32)
        im = g[here[0], here[1], 1].astype(F32)
        mag = jnp.sqrt(re * re + im * im)
        part = jnp.sum(mag, axis=0, keepdims=True)
        if n == 0:
            lvall[t] = part
        else:
            lvall[t] = lvall[t] + part

    def near(n):
        here = block(n, 3)
        arrive(here)
        if n % 2 == 0:
            forward(here, up)
        forward(here, sib)
        here = block(n, 1)
        arrive(here)
        if n % 2 == 1:
            forward(here, down)
        forward(here, sib)

    def far(n):
        here = block(n, 2)
        arrive(here)
        forward(here, sib)

    for n in range(8):
        own(n)
        if n == 7:
            levels = [send(lvall.at[t], lvall.at[t], t_peer(d)) for d in range(1, 8)]
        if n >= 1:
            near(n - 1)
        if n >= 2:
            far(n - 2)
    qcopy.wait_recv()
    row = pl.ds(2 * z + x % 2, 1)
    use_ref[...] = jnp.where(x // 2 == core, qual_ref[row], qbuf[row]).astype(F32)
    for copy in levels:
        copy.wait_recv()
    level = lvall[0]
    for n in range(1, 8):
        level = level + lvall[n]
    add_ref[...] = 0.5 * (level / F + 1e-05)
    acc[...] = jnp.zeros_like(acc)
    lane = lax.broadcasted_iota(jnp.int32, (FB, TILE), 1)

    def compute(gi):
        def whiten(k, carry):
            for m in range(NEED):
                cols = tile_at(jnp.minimum(t + m, 7))
                live = jnp.where(t + m < 8, 1.0, 0.0)
                re = g[gi, k, 0, :, cols].astype(F32)
                im = g[gi, k, 1, :, cols].astype(F32)
                mag = jnp.sqrt(re * re + im * im)
                factor = (use_ref[:, cols] * live) / (mag + add_ref[:, cols])
                w[m, 0, k] = (re * factor).astype(BF)
                w[m, 1, k] = (im * factor).astype(BF)
            return carry

        lax.fori_loop(0, 8, whiten, 0)

        def cross(k, carry):
            rows = pl.ds(pl.multiple_of(k * FB, FB), FB)
            own_re = w[0, 0, k].astype(F32)
            own_im = w[0, 1, k].astype(F32)
            for j in range(NOFF):
                whole = off_ref[j] // 8
                rest = off_ref[j] % 8 * 16
                keep = lane >= rest
                back = (TILE - rest) % TILE
                far_re = jnp.where(keep, w[whole, 0, k].astype(F32), w[whole + 1, 0, k].astype(F32))
                far_im = jnp.where(keep, w[whole, 1, k].astype(F32), w[whole + 1, 1, k].astype(F32))
                far_re = pltpu.roll(far_re, back, 1)
                far_im = pltpu.roll(far_im, back, 1)
                xmat[rows, j * TILE : (j + 1) * TILE] = (own_re * far_re + own_im * far_im).astype(BF)
                xmat[rows, 512 + j * TILE : 512 + (j + 1) * TILE] = (own_im * far_re - own_re * far_im).astype(BF)
            return carry

        lax.fori_loop(0, 8, cross, 0)
        acc[...] += jnp.dot(tab_ref[gi], xmat[...], preferred_element_type=F32)

    w[NEED] = jnp.zeros_like(w[NEED])

    def turn(i, carry):
        @pl.when(i == 1)
        def _():
            near(7)
            far(6)

        @pl.when(i == 3)
        def _():
            far(7)

        dy = jnp.where(i < 2, 0, jnp.where(i >= 6, 2, jnp.where(i % 2 == 0, 3, 1)))
        other = jnp.where((i == 1) | (i == 4) | (i == 5) | (i == 7), 1, 0)
        gi = (y + dy) % 4 * 2 + (par + other) % 2

        @pl.when(other == 1)
        def _():
            for k in range(8):
                arrive((gi, k))

        compute(gi)
        return carry

    lax.fori_loop(0, 8, turn, 0)

    scale = 1.0 / math.sqrt(F)

    def phases(j):
        left = tile_at(j)
        right = tile_at(j + NOFF)
        a = acc[:HALF, left]
        b = acc[HALF:, right]
        c = acc[HALF:, left]
        d = acc[:HALF, right]
        pos_r = (a - b) * scale
        neg_r = (a + b) * scale
        pos_q = (d + c) * scale
        neg_q = (d - c) * scale
        pos_p = pos_r * pos_r + pos_q * pos_q
        neg_p = neg_r * neg_r + neg_q * neg_q
        mean = jnp.sum(pos_p + neg_p, axis=0, keepdims=True) / LAGS
        floor = 0.25 * (mean + 1e-06)
        pos_d = jnp.sqrt(pos_p + floor)
        neg_d = jnp.sqrt(neg_p + floor)
        p[0, 0, j] = pos_r
        p[1, 0, j] = neg_r
        p[0, 1, j] = pos_r / pos_d
        p[1, 1, j] = neg_r / neg_d
        p[0, 2, j] = pos_q / pos_d
        p[1, 2, j] = neg_q / neg_d

    right, left, across = (x + 1) % 4, (x + 3) % 4, (x + 2) % 4
    phases(across)
    to_right = send(p.at[0, :, across], ring.at[0], x_peer(1))
    to_left = send(p.at[1, :, across], ring.at[1], x_peer(3))
    phases(right)
    plain_right = send(p.at[1, :, right], ringin.at[0], x_peer(1))
    phases(left)
    plain_left = send(p.at[0, :, left], ringin.at[1], x_peer(3))
    phases(x)
    to_right.wait_recv()
    ringsum[0] = ring[0] + p[0, :, right]
    both_right = send(ringsum.at[0], ringin.at[2], x_peer(1))
    to_left.wait_recv()
    ringsum[1] = ring[1] + p[1, :, left]
    both_left = send(ringsum.at[1], ringin.at[3], x_peer(3))
    plain_right.wait_recv()
    plain_left.wait_recv()
    both_right.wait_recv()
    zacc[0] = (p[0, :, x] + ringin[1]) + ringin[2]
    both_left.wait_recv()
    zacc[1] = (p[1, :, x] + ringin[0]) + ringin[3]

    def lag_rows(where):
        return pl.ds(pl.multiple_of(where * 16, 16), 16)

    copies = [
        send(zacc.at[:, :, lag_rows((zall + d) % 8)], zbuf.at[d - 1], z_peer(d)) for d in (4, 3, 5, 2, 6, 1, 7)
    ]
    total = zacc[:, :, lag_rows(zall)]
    for copy in copies:
        copy.wait_recv()
    for d in range(7):
        total = total + zbuf[d]
    linear = total[:, 0] / WINDOWS
    real = total[:, 1] / WINDOWS
    imag = total[:, 2] / WINDOWS
    st[t] = linear * (real * real + imag * imag)

    copies = [send(st.at[t], st.at[t], t_peer(d)) for d in range(1, 8)]
    for copy in copies:
        copy.wait_recv()
    shift = off_ref[x]
    whole = shift // 8
    rest = shift % 8 * 16
    wide = lax.broadcasted_iota(jnp.int32, (2, 16, TILE), 2)
    pieces = []
    for n in range(4):
        tile = 2 * n + y // 2
        first = tile - whole
        a = jnp.where(first >= 0, st[jnp.maximum(first, 0)], 0.0)
        b = jnp.where(first >= 1, st[jnp.maximum(first - 1, 0)], 0.0)
        rev = pltpu.roll(jnp.where(wide < TILE - rest, a, b).reshape(32, TILE), rest, 1).reshape(2, 16, TILE)
        ahead = st[tile]
        pieces.append(ahead[0] + rev[1])
        pieces.append(ahead[1] + rev[0])
    tbuf[...] = jnp.concatenate(pieces, axis=0).T

    def channel_rows(where):
        return pl.ds(pl.multiple_of(y % 2 * 64 + where * 16, 16), 16)

    copies = [send(tbuf.at[channel_rows((x + d) % 4)], jbuf.at[x], x_peer(d)) for d in (1, 2, 3)]
    jbuf[x] = tbuf[channel_rows(x)]
    for copy in copies:
        copy.wait_recv()
    group = lax.broadcasted_iota(jnp.int32, (16, TILE), 1) // 32
    for n in range(4):
        merged = jnp.zeros((16, TILE), F32)
        for j in range(NOFF):
            merged = jnp.where(group == j, pltpu.roll(jbuf[j], (32 * (j - n)) % TILE, 1), merged)
        mbuf[n] = merged
    copies = [send(mbuf.at[(zall + d) % 4], rbuf.at[zall], z_peer(d)) for d in (4, 3, 5, 2, 6, 1, 7)]
    rbuf[zall] = mbuf[zall % 4]
    for copy in copies:
        copy.wait_recv()
    span = lax.broadcasted_iota(jnp.int32, (16, TILE), 1) // 16
    for j in range(NOFF):
        for s in range(2):
            merged = jnp.zeros((16, TILE), F32)
            for n in range(8):
                merged = jnp.where(span == n, pltpu.roll(rbuf[n], (16 * n - 32 * j - 16 * s) % TILE, 1), merged)
            out_ref[j, s] = merged
    for n in sent:
        pltpu.make_async_remote_copy(
            src_ref=g.at[0, 0],
            dst_ref=g.at[0, 0],
            send_sem=gsend.at[n],
            recv_sem=grecv.at[0, 0],
            device_id=sib,
            device_id_type=MESH,
        ).wait_send()
    for copy in started:
        copy.wait_send()


def whole_window(offsets, spectra, quality, table):
    vmem = pl.BlockSpec(memory_space=pltpu.VMEM)
    return pl.pallas_call(
        window_kernel,
        name="whole_window",
        out_shape=jax.ShapeDtypeStruct((NOFF, 2, 16, TILE), F32),
        in_specs=[pl.BlockSpec(memory_space=pltpu.SMEM), pl.BlockSpec(memory_space=pl.ANY), vmem, vmem],
        out_specs=vmem,
        scratch_shapes=[
            pltpu.VMEM((8, 8, 2, FB, NCH), BF),
            pltpu.VMEM((8, NCH), jnp.int32),
            pltpu.VMEM((8, 1, NCH), F32),
            pltpu.VMEM((1, NCH), F32),
            pltpu.VMEM((1, NCH), F32),
            pltpu.VMEM((NEED + 1, 2, 8, FB, TILE), BF),
            pltpu.VMEM((GROUP, 2 * NOFF * TILE), BF),
            pltpu.VMEM((2 * HALF, 2 * NOFF * TILE), F32),
            pltpu.VMEM((2, 3, NOFF, HALF, TILE), F32),
            pltpu.VMEM((2, 3, HALF, TILE), F32),
            pltpu.VMEM((2, 3, HALF, TILE), F32),
            pltpu.VMEM((4, 3, HALF, TILE), F32),
            pltpu.VMEM((2, 3, HALF, TILE), F32),
            pltpu.VMEM((7, 2, 3, 16, TILE), F32),
            pltpu.VMEM((8, 2, 16, TILE), F32),
            pltpu.VMEM((TILE, TILE), F32),
            pltpu.VMEM((NOFF, 16, TILE), F32),
            pltpu.VMEM((4, 16, TILE), F32),
            pltpu.VMEM((8, 16, TILE), F32),
            pltpu.SemaphoreType.DMA((64,)),
            pltpu.SemaphoreType.DMA((8, 8)),
            pltpu.SemaphoreType.DMA((40,)),
            pltpu.SemaphoreType.DMA((40,)),
        ],
        compiler_params=pltpu.CompilerParams(collective_id=0, has_side_effects=True),
    )(offsets, spectra, quality, table)


def shards(spectra, quality, offsets):
    table = jnp.asarray(half_table()).astype(BF)
    halves = whole_window(offsets, spectra, quality, table)
    late = jnp.transpose(halves[:, 0], (1, 0, 2))
    early = jnp.flip(jnp.transpose(halves[:, 1], (1, 0, 2)), axis=2)
    return jnp.concatenate([early, late], axis=2)


def solution(mesh):
    return jax.shard_map(
        shards,
        mesh=mesh,
        in_specs=(P(None, "tm", "chan", None), P("tm", None), P()),
        out_specs=P("chan", None, None),
        check_vma=False,
    )
```

time: 858 us -> 112 us (0.13)
  waiting for transfers between devices: 721 us -> 0 us
  Pallas kernels: 0 us -> 111 us
  starting transfers between devices: 55.1 us -> 0 us
  local copies, waits for them, and re-layouts: 38.9 us -> 1.54 us
  other arithmetic: 21.3 us -> 0.01 us
  between operations: 13.7 us -> 0.01 us
    ppermute x12 -> x0, waiting for transfers between devices: 631 us -> none  [shifted(): lax.ppermute(value, axis, [(source, source + steps) for source in range(l...]
    pallas_call x0 -> x1, Pallas kernels: none -> 111 us  [whole_window(): pl.pallas_call(window_kernel, name='whole_window', out_shape=jax.ShapeDty...]
    psum x1 -> x0, waiting for transfers between devices: 63.1 us -> none  [shards(): totals = lax.psum((linear_sum, real_sum, imag_sum), 'tm')]
    ppermute x12 -> x0, starting transfers between devices: 42.6 us -> none  [shifted(): lax.ppermute(value, axis, [(source, source + steps) for source in range(l...]
    all_to_all x1 -> x0, waiting for transfers between devices: 26.5 us -> none  [shards(): lax.all_to_all(spectra, 'chan', split_axis=3, concat_axis=2, tiled=True)]
    unnamed x7 -> x0, local copies, waits for them, and re-layouts: 16.6 us -> none
    convert_element_type x4 -> x0, local copies, waits for them, and re-layouts: 14 us -> none  [the longest x2 7.63 us: whiten_channels(): real_part = grouped[0].astype(jnp.float32)]
    all_to_all x1 -> x0, starting transfers between devices: 12.5 us -> none  [shards(): lax.all_to_all(spectra, 'chan', split_axis=3, concat_axis=2, tiled=True)]
  transfers between devices with their start and end apart: 14 -> 0, of which waited for: 14 -> 0; matrix products, arithmetic and copies ran while one was open for 1% -> 0% of each run, Pallas kernels for 0% -> 0%
where the time goes in v2:
time: 112 us
  Pallas kernels  111 us (99%)
  local copies, waits for them, and re-layouts  1.54 us (1%)
    pallas_call x1, Pallas kernels, whole_window(): pl.pallas_call(window_kernel, name='whole_window', out_shape=jax.ShapeDty...  111 us

profile of v2, /device:TPU:1, one launch (start us, length us, event | category | flops | bytes accessed | tf_op | source)
XLA Modules:
  0.0 112.2 jit_solution(17806497234823382937)
XLA Ops:
  0.0 110.7 %whole_window.1 = f32[4,2,16,128]{3,2,1,0:T(8,128)} custom-call(s32[4]{0:T(128)} %off_ref.1, bf16[2,8,32,1024]{3,2,1,0:T(8,128)(2,1)} %spec_ref.1, s32[8,1024]{1,0:T(8,128)} %qual_ref.1, bf16[8,256,256]{2,1,0:T(8,128)(2,1)} %constant.4.tab_ref), custom_call_target="tpu_custom_call" | custom-call | tf_op jit(solution)/shard_map/whole_window/pallas_call | solution.py:372
  110.7 0.8 slice_bitcast_fusion.1
  111.5 0.1 rev.4
  111.6 0.7 copy.6
  (1 shorter events, 0.0 us)

commit v3 on v2

--- a/solution.py
+++ b/solution.py
@@ -16,8 +16,8 @@
 WINDOWS = 32
 NCH = 1024
 TILE = 128
+FB = 32
 NEED = 5
-FB = 32
 GROUP = 256
 BF = jnp.bfloat16
 F32 = jnp.float32
@@ -30,7 +30,7 @@
 
 
 def half_table():
-    y, par, z, half, low = np.meshgrid(*(np.arange(n) for n in (4, 2, 4, 2, FB)), indexing="ij")
+    z, half, y, par, low = np.meshgrid(*(np.arange(n) for n in (4, 2, 4, 2, FB)), indexing="ij")
     freq = ((z * 16 + y * 4 + 2 * half + par) * FB + low).reshape(8, 1, GROUP).astype(np.int64)
     lag = (2 * np.arange(HALF, dtype=np.int64) + 1)[None, :, None]
     angle = ((freq * lag) % (4 * F)).astype(np.float64) * (2.0 * math.pi / (4 * F))
@@ -42,10 +42,10 @@
 
 
 def window_kernel(
-    off_ref, spec_ref, qual_ref, tab_ref, out_ref,
-    g, qbuf, lvall, add_ref, use_ref, w, xmat, acc, p,
+    off_ref, spec_ref, qual_ref, tab_hbm, out_ref,
+    spec, qown, qbuf, tab, g, lvown, lvin, lvall, add_ref, use_ref, w, xmat, acc, p,
     ring, ringsum, ringin, zacc, zbuf, st, tbuf, jbuf, mbuf, rbuf,
-    gsend, grecv, send_sem, recv_sem,
+    local_sem, own_sem, row_sem, gsend, grecv, send_sem, recv_sem,
 ):
     z, y, x, zh, core = place()
     chan = z * 16 + y * 4 + x
@@ -72,6 +72,12 @@
     zs = [z, mate, 3 - z, 3 - mate]
     spots = [(zs[k], xh) for k in range(4) for xh in (0, 1)]
 
+    loads = [
+        pltpu.make_async_copy(src, dst, local_sem.at[n])
+        for n, (src, dst) in enumerate(((spec_ref, spec), (qual_ref, qown), (tab_hbm, tab)))
+    ]
+    for copy in loads:
+        copy.start()
     barrier = pltpu.get_barrier_semaphore()
     greet = [(zt * 16 + y * 4 + 2 * xh + par, zh * 2 + x // 2) for zt, xh in spots]
     greet += [x_peer(d) for d in (1, 2, 3)]
@@ -79,35 +85,18 @@
     greet += [t_peer(d) for d in range(1, 8)]
     for there in greet:
         pl.semaphore_signal(barrier, inc=1, device_id=there, device_id_type=MESH)
+    loads[0].wait()
+
+    def measure(i, carry):
+        re = spec[0, i].astype(F32)
+        im = spec[1, i].astype(F32)
+        lvown[i] = jnp.sum(jnp.sqrt(re * re + im * im), axis=0, keepdims=True)
+        return carry
+
+    lax.fori_loop(0, 8, measure, 0)
     pl.semaphore_wait(barrier, len(greet))
 
-    sent = []
     started = []
-
-    def put(src, where, there):
-        copy = pltpu.make_async_remote_copy(
-            src_ref=src,
-            dst_ref=g.at[where[0], where[1]],
-            send_sem=gsend.at[len(sent)],
-            recv_sem=grecv.at[where[0], where[1]],
-            device_id=there,
-            device_id_type=MESH,
-        )
-        copy.start()
-        sent.append(len(sent))
-
-    def forward(where, there):
-        put(g.at[where[0], where[1]], where, there)
-
-    def arrive(where):
-        pltpu.make_async_remote_copy(
-            src_ref=g.at[where[0], where[1]],
-            dst_ref=g.at[where[0], where[1]],
-            send_sem=gsend.at[0],
-            recv_sem=grecv.at[where[0], where[1]],
-            device_id=sib,
-            device_id_type=MESH,
-        ).wait_recv()
 
     def send(src, dst, there):
         copy = pltpu.make_async_remote_copy(
@@ -122,96 +111,165 @@
         started.append(copy)
         return copy
 
-    home = (y * 2 + x % 2, z * 2 + x // 2)
-    for zt, low in spots:
-        put(
-            spec_ref.at[:, 2 * zt + low],
-            home,
-            (zt * 16 + y * 4 + low + 2 * core, zh * 2 + (x + low + 1 + core) % 2),
+    landings = [
+        (2 * zt + low, (zt * 16 + y * 4 + low + 2 * core, zh * 2 + (x + low + 1 + core) % 2)) for zt, low in spots
+    ]
+    home = z * 2 + x // 2
+    first_hop = []
+    for n, (i, there) in enumerate(landings):
+        first_hop.append((lvown.at[i], lvin.at[home], row_sem.at[0, n], row_sem.at[1, home], there))
+    for n, (i, there) in enumerate(landings):
+        first_hop.append((spec_ref.at[:, i], g.at[home, y * 2 + x % 2], own_sem.at[0, n], own_sem.at[1, home], there))
+    first_hop = [
+        pltpu.make_async_remote_copy(
+            src_ref=src, dst_ref=dst, send_sem=ssem, recv_sem=rsem, device_id=there, device_id_type=MESH
         )
-    qcopy = send(qual_ref, qbuf, sib)
-
-    def block(n, dy):
-        return ((y + dy) % 4 * 2 + par, spots[n][0] * 2 + spots[n][1])
-
-    def own(n):
-        here = block(n, 0)
-        arrive(here)
-        forward(here, up)
-        forward(here, down)
-        forward(here, sib)
-        re = g[here[0], here[1], 0].astype(F32)
-        im = g[here[0], here[1], 1].astype(F32)
-        mag = jnp.sqrt(re * re + im * im)
-        part = jnp.sum(mag, axis=0, keepdims=True)
-        if n == 0:
-            lvall[t] = part
-        else:
-            lvall[t] = lvall[t] + part
-
-    def near(n):
-        here = block(n, 3)
-        arrive(here)
-        if n % 2 == 0:
-            forward(here, up)
-        forward(here, sib)
-        here = block(n, 1)
-        arrive(here)
-        if n % 2 == 1:
-            forward(here, down)
-        forward(here, sib)
-
-    def far(n):
-        here = block(n, 2)
-        arrive(here)
-        forward(here, sib)
-
-    for n in range(8):
-        own(n)
-        if n == 7:
-            levels = [send(lvall.at[t], lvall.at[t], t_peer(d)) for d in range(1, 8)]
-        if n >= 1:
-            near(n - 1)
-        if n >= 2:
-            far(n - 2)
+        for src, dst, ssem, rsem, there in first_hop
+    ]
+    for copy in first_hop[:8]:
+        copy.start()
+    loads[1].wait()
+    qcopy = send(qown, qbuf, sib)
+    for copy in first_hop[8:]:
+        copy.start()
+
+    def landed(ref, sem):
+        pltpu.make_async_remote_copy(
+            src_ref=ref, dst_ref=ref, send_sem=own_sem.at[0, 0], recv_sem=sem, device_id=sib, device_id_type=MESH
+        ).wait_recv()
+
+    for k in range(8):
+        landed(lvin.at[k], row_sem.at[1, k])
+    part = lvin[0]
+    for k in range(1, 8):
+        part = part + lvin[k]
+    lvall[t] = part
+    levels = [send(lvall.at[t], lvall.at[t], t_peer(d)) for d in range(1, 8)]
     qcopy.wait_recv()
     row = pl.ds(2 * z + x % 2, 1)
-    use_ref[...] = jnp.where(x // 2 == core, qual_ref[row], qbuf[row]).astype(F32)
+    use_ref[...] = jnp.where(x // 2 == core, qown[row], qbuf[row]).astype(F32)
+    acc[...] = jnp.zeros_like(acc)
+    w[NEED] = jnp.zeros_like(w[NEED])
     for copy in levels:
         copy.wait_recv()
     level = lvall[0]
     for n in range(1, 8):
         level = level + lvall[n]
     add_ref[...] = 0.5 * (level / F + 1e-05)
-    acc[...] = jnp.zeros_like(acc)
+    loads[2].wait()
+
+    def quad(gi, m, q):
+        return g.at[gi, m, :, :, pl.ds(pl.multiple_of(q * 256, 256), 256)]
+
+    def hop(gi, m, q, kind, n, there):
+        return pltpu.make_async_remote_copy(
+            src_ref=quad(gi, m, q),
+            dst_ref=quad(gi, m, q),
+            send_sem=gsend.at[kind, n, q],
+            recv_sem=grecv.at[gi, m, q],
+            device_id=there,
+            device_id_type=MESH,
+        )
+
+    def forward(gi, m, span, kind, n, there):
+        def one(q, carry):
+            hop(gi, m, q, kind, n, there).start()
+            return carry
+
+        lax.fori_loop(span[0], span[1] + 1, one, 0)
+
+    def arrive(gi, m, span):
+        def one(q, carry):
+            hop(gi, m, q, 0, 0, sib).wait_recv()
+            return carry
+
+        lax.fori_loop(span[0], span[1] + 1, one, 0)
+
+    def needs(at):
+        return at, jnp.minimum(at + 2, 3)
+
+    def upward(at, relay):
+        lone = needs(at)
+        return jnp.where(relay, jnp.where(at == 3, 0, at), lone[0]), jnp.where(relay, 3, lone[1])
+
+    def downward(at, relay):
+        lone = needs(at)
+        return jnp.where(relay, jnp.maximum(at - 1, 0), lone[0]), jnp.where(relay, 3, lone[1])
+
+    above, below, beyond = (y + 1) % 4, (y + 3) % 4, (y + 2) % 4
+    mine = needs(y)
+
+    def group_of(n):
+        k = n // 2
+        zt = jnp.where(k == 0, zs[0], jnp.where(k == 1, zs[1], jnp.where(k == 2, zs[2], zs[3])))
+        return zt * 2 + n % 2
+
+    def own(n):
+        gi = group_of(n)
+        m = y * 2 + par
+        landed(g.at[gi, m], own_sem.at[1, gi])
+        for c in range(8):
+            cols = slice(c * TILE, (c + 1) * TILE)
+            re = g[gi, m, 0, :, cols].astype(F32)
+            im = g[gi, m, 1, :, cols].astype(F32)
+            factor = use_ref[:, cols] / (jnp.sqrt(re * re + im * im) + add_ref[:, cols])
+            g[gi, m, 0, :, cols] = (re * factor).astype(BF)
+            g[gi, m, 1, :, cols] = (im * factor).astype(BF)
+        even = n % 2 == 0
+        forward(gi, m, upward(above, even), 0, n, up)
+        forward(gi, m, downward(below, jnp.logical_not(even)), 1, n, down)
+        forward(gi, m, mine, 2, n, sib)
+
+    def near(n):
+        gi = group_of(n)
+        even = n % 2 == 0
+        m = below * 2 + par
+        arrive(gi, m, upward(y, even))
+
+        @pl.when(even)
+        def _():
+            forward(gi, m, needs(above), 3, n, up)
+
+        forward(gi, m, mine, 4, n, sib)
+        m = above * 2 + par
+        arrive(gi, m, downward(y, jnp.logical_not(even)))
+
+        @pl.when(jnp.logical_not(even))
+        def _():
+            forward(gi, m, needs(below), 3, n, down)
+
+        forward(gi, m, mine, 5, n, sib)
+
+    def far(n):
+        gi = group_of(n)
+        m = beyond * 2 + par
+        arrive(gi, m, mine)
+        forward(gi, m, mine, 6, n, sib)
+
     lane = lax.broadcasted_iota(jnp.int32, (FB, TILE), 1)
 
-    def compute(gi):
-        def whiten(k, carry):
-            for m in range(NEED):
-                cols = tile_at(jnp.minimum(t + m, 7))
-                live = jnp.where(t + m < 8, 1.0, 0.0)
-                re = g[gi, k, 0, :, cols].astype(F32)
-                im = g[gi, k, 1, :, cols].astype(F32)
-                mag = jnp.sqrt(re * re + im * im)
-                factor = (use_ref[:, cols] * live) / (mag + add_ref[:, cols])
-                w[m, 0, k] = (re * factor).astype(BF)
-                w[m, 1, k] = (im * factor).astype(BF)
-            return carry
-
-        lax.fori_loop(0, 8, whiten, 0)
-
-        def cross(k, carry):
-            rows = pl.ds(pl.multiple_of(k * FB, FB), FB)
-            own_re = w[0, 0, k].astype(F32)
-            own_im = w[0, 1, k].astype(F32)
+    def compute(n):
+        gi = group_of(n)
+        for m in range(4):
+            arrive(gi, m * 2 + 1 - par, mine)
+
+        for a in range(NEED):
+            cols = tile_at(jnp.minimum(t + a, 7))
+            for part in range(2):
+                value = g[gi, :, part, :, cols]
+                w[a, part] = jnp.where(t + a < 8, value, jnp.zeros_like(value))
+
+        def cross(m, carry):
+            rows = pl.ds(pl.multiple_of(m * FB, FB), FB)
+            own_re = w[0, 0, m].astype(F32)
+            own_im = w[0, 1, m].astype(F32)
             for j in range(NOFF):
                 whole = off_ref[j] // 8
                 rest = off_ref[j] % 8 * 16
                 keep = lane >= rest
                 back = (TILE - rest) % TILE
-                far_re = jnp.where(keep, w[whole, 0, k].astype(F32), w[whole + 1, 0, k].astype(F32))
-                far_im = jnp.where(keep, w[whole, 1, k].astype(F32), w[whole + 1, 1, k].astype(F32))
+                far_re = jnp.where(keep, w[whole, 0, m].astype(F32), w[whole + 1, 0, m].astype(F32))
+                far_im = jnp.where(keep, w[whole, 1, m].astype(F32), w[whole + 1, 1, m].astype(F32))
                 far_re = pltpu.roll(far_re, back, 1)
                 far_im = pltpu.roll(far_im, back, 1)
                 xmat[rows, j * TILE : (j + 1) * TILE] = (own_re * far_re + own_im * far_im).astype(BF)
@@ -219,33 +277,18 @@
             return carry
 
         lax.fori_loop(0, 8, cross, 0)
-        acc[...] += jnp.dot(tab_ref[gi], xmat[...], preferred_element_type=F32)
-
-    w[NEED] = jnp.zeros_like(w[NEED])
+        acc[...] += jnp.dot(tab[gi], xmat[...], preferred_element_type=F32)
 
     def turn(i, carry):
-        @pl.when(i == 1)
-        def _():
-            near(7)
-            far(6)
-
-        @pl.when(i == 3)
-        def _():
-            far(7)
-
-        dy = jnp.where(i < 2, 0, jnp.where(i >= 6, 2, jnp.where(i % 2 == 0, 3, 1)))
-        other = jnp.where((i == 1) | (i == 4) | (i == 5) | (i == 7), 1, 0)
-        gi = (y + dy) % 4 * 2 + (par + other) % 2
-
-        @pl.when(other == 1)
-        def _():
-            for k in range(8):
-                arrive((gi, k))
-
-        compute(gi)
+        for stage, first in ((own, 0), (near, 1), (far, 2), (compute, 3)):
+
+            @pl.when((i >= first) & (i < first + 8))
+            def _(stage=stage, first=first):
+                stage(i - first)
+
         return carry
 
-    lax.fori_loop(0, 8, turn, 0)
+    lax.fori_loop(0, 11, turn, 0)
 
     scale = 1.0 / math.sqrt(F)
 
@@ -354,15 +397,25 @@
             for n in range(8):
                 merged = jnp.where(span == n, pltpu.roll(rbuf[n], (16 * n - 32 * j - 16 * s) % TILE, 1), merged)
             out_ref[j, s] = merged
-    for n in sent:
-        pltpu.make_async_remote_copy(
-            src_ref=g.at[0, 0],
-            dst_ref=g.at[0, 0],
-            send_sem=gsend.at[n],
-            recv_sem=grecv.at[0, 0],
-            device_id=sib,
-            device_id_type=MESH,
-        ).wait_send()
+    for copy in first_hop:
+        copy.wait_send()
+
+    def sent(n, carry):
+        even = n % 2 == 0
+        onward = jnp.where(even, above, below)
+        spans = (
+            upward(above, even), downward(below, jnp.logical_not(even)), mine, needs(onward), mine, mine, mine,
+        )
+        for kind, span in enumerate(spans):
+
+            def one(q, inner, kind=kind):
+                hop(0, 0, q, kind, n, sib).wait_send()
+                return inner
+
+            lax.fori_loop(span[0], span[1] + 1, one, 0)
+        return carry
+
+    lax.fori_loop(0, 8, sent, 0)
     for copy in started:
         copy.wait_send()
 
@@ -373,11 +426,16 @@
         window_kernel,
         name="whole_window",
         out_shape=jax.ShapeDtypeStruct((NOFF, 2, 16, TILE), F32),
-        in_specs=[pl.BlockSpec(memory_space=pltpu.SMEM), pl.BlockSpec(memory_space=pl.ANY), vmem, vmem],
+        in_specs=[pl.BlockSpec(memory_space=pltpu.SMEM)] + [pl.BlockSpec(memory_space=pl.ANY)] * 3,
         out_specs=vmem,
         scratch_shapes=[
+            pltpu.VMEM((2, 8, FB, NCH), BF),
+            pltpu.VMEM((8, NCH), jnp.int32),
+            pltpu.VMEM((8, NCH), jnp.int32),
+            pltpu.VMEM((8, 2 * HALF, GROUP), BF),
             pltpu.VMEM((8, 8, 2, FB, NCH), BF),
-            pltpu.VMEM((8, NCH), jnp.int32),
+            pltpu.VMEM((8, 1, NCH), F32),
+            pltpu.VMEM((8, 1, NCH), F32),
             pltpu.VMEM((8, 1, NCH), F32),
             pltpu.VMEM((1, NCH), F32),
             pltpu.VMEM((1, NCH), F32),
@@ -395,8 +453,11 @@
             pltpu.VMEM((NOFF, 16, TILE), F32),
             pltpu.VMEM((4, 16, TILE), F32),
             pltpu.VMEM((8, 16, TILE), F32),
-            pltpu.SemaphoreType.DMA((64,)),
-            pltpu.SemaphoreType.DMA((8, 8)),
+            pltpu.SemaphoreType.DMA((3,)),
+            pltpu.SemaphoreType.DMA((2, 8)),
+            pltpu.SemaphoreType.DMA((2, 8)),
+            pltpu.SemaphoreType.DMA((7, 8, 4)),
+            pltpu.SemaphoreType.DMA((8, 8, 4)),
             pltpu.SemaphoreType.DMA((40,)),
             pltpu.SemaphoreType.DMA((40,)),
         ],

time: 112 us -> 104 us (0.929)
  Pallas kernels: 111 us -> 102 us
    pallas_call x1, Pallas kernels: 111 us -> 102 us  [whole_window(): pl.pallas_call(window_kernel, name='whole_window', out_shape=jax.ShapeDty...]
where the time goes in v3:
time: 104 us
  Pallas kernels  102 us (98%)
  local copies, waits for them, and re-layouts  1.54 us (1%)
    pallas_call x1, Pallas kernels, whole_window(): pl.pallas_call(window_kernel, name='whole_window', out_shape=jax.ShapeDty...  102 us

profile of v3, /device:TPU:1, one launch (start us, length us, event | category | flops | bytes accessed | tf_op | source)
XLA Modules:
  0.0 103.9 jit_solution(6983259867173370173)
XLA Ops:
  0.0 102.3 %whole_window.1 = f32[4,2,16,128]{3,2,1,0:T(8,128)} custom-call(s32[4]{0:T(128)} %off_ref.1, bf16[2,8,32,1024]{3,2,1,0:T(8,128)(2,1)} %spec_ref.1, s32[8,1024]{1,0:T(8,128)} %qual_ref.1, bf16[8,256,256]{2,1,0:T(8,128)(2,1)} %constant.4.tab_hbm), custom_call_target="tpu_custom_call" | custom-call | tf_op jit(solution)/shard_map/whole_window/pallas_call | solution.py:425
  102.3 0.8 slice_bitcast_fusion.1
  103.1 0.1 rev.4
  103.2 0.7 copy.6
  (1 shorter events, 0.0 us)

commit v4 on v3

v4 whole, which is shorter than its diff:
```python
import math

import jax
import jax.numpy as jnp
import numpy as np
from jax import lax
from jax.experimental import pallas as pl
from jax.experimental.pallas import tpu as pltpu
from jax.sharding import PartitionSpec as P

MESH = pl.DeviceIdType.MESH
F = 2048
LAGS = 256
HALF = 128
NOFF = 4
WINDOWS = 32
NCH = 1024
TILE = 128
FB = 32
NEED = 5
RAW = 4
GROUP = 256
BF = jnp.bfloat16
F32 = jnp.float32


def place():
    chan = lax.axis_index("chan")
    tm = lax.axis_index("tm")
    return chan // 16, (chan // 4) % 4, chan % 4, tm // 2, tm % 2


def half_table():
    z, half, y, par, low = np.meshgrid(*(np.arange(n) for n in (4, 2, 4, 2, FB)), indexing="ij")
    freq = ((z * 16 + y * 4 + 2 * half + par) * FB + low).reshape(8, 1, GROUP).astype(np.int64)
    lag = (2 * np.arange(HALF, dtype=np.int64) + 1)[None, :, None]
    angle = ((freq * lag) % (4 * F)).astype(np.float64) * (2.0 * math.pi / (4 * F))
    return np.concatenate([np.cos(angle), np.sin(angle)], axis=1).astype(np.float32)


def tile_at(where):
    return pl.ds(pl.multiple_of(where * TILE, TILE), TILE)


def window_kernel(
    off_ref, spec_ref, qual_ref, tab_hbm, out_ref,
    spec, qown, qbuf, tab, g, lvown, lvin, lvall, add_ref, use_ref, w, xmat, acc, p,
    ring, ringsum, ringin, zacc, zbuf, st, tbuf, jbuf, mbuf, rbuf,
    local_sem, own_recv, own_send, row_sem, gsend, grecv, gsib, send_sem, recv_sem,
):
    z, y, x, zh, core = place()
    chan = z * 16 + y * 4 + x
    tm = zh * 2 + core
    sib = (chan, zh * 2 + 1 - core)
    t = y * 2 + core
    zall = zh * 4 + z
    par = (core + x + 1 + x // 2) % 2
    up = (z * 16 + ((y + 1) % 4) * 4 + x, tm)
    down = (z * 16 + ((y + 3) % 4) * 4 + x, tm)

    def x_peer(d):
        return (z * 16 + y * 4 + (x + d) % 4, tm)

    def z_peer(d):
        there = (zall + d) % 8
        return (there % 4 * 16 + y * 4 + x, there // 4 * 2 + core)

    def t_peer(d):
        there = (t + d) % 8
        return (z * 16 + there // 2 * 4 + x, zh * 2 + there % 2)

    mate = z + 1 - 2 * (z % 2)
    zs = [z, mate, 3 - z, 3 - mate]
    spots = [(zs[k], xh) for k in range(4) for xh in (0, 1)]

    loads = [
        pltpu.make_async_copy(src, dst, local_sem.at[n])
        for n, (src, dst) in enumerate(((spec_ref, spec), (qual_ref, qown), (tab_hbm, tab)))
    ]
    for copy in loads:
        copy.start()
    barrier = pltpu.get_barrier_semaphore()
    greet = [(zt * 16 + y * 4 + 2 * xh + par, zh * 2 + x // 2) for zt, xh in spots]
    greet += [x_peer(d) for d in (1, 2, 3)]
    greet += [z_peer(d) for d in range(1, 8)]
    greet += [t_peer(d) for d in range(1, 8)]
    for there in greet:
        pl.semaphore_signal(barrier, inc=1, device_id=there, device_id_type=MESH)
    pl.semaphore_wait(barrier, len(greet))

    def remote(src, dst, ssem, rsem, there):
        return pltpu.make_async_remote_copy(
            src_ref=src, dst_ref=dst, send_sem=ssem, recv_sem=rsem, device_id=there, device_id_type=MESH
        )

    def send(src, dst, out_sem, in_sem, there):
        remote(src, dst, send_sem.at[out_sem], recv_sem.at[in_sem], there).start()

    def received(ref, in_sem):
        remote(ref, ref, send_sem.at[0], recv_sem.at[in_sem], sib).wait_recv()

    def gone(ref, sem):
        remote(ref, ref, sem, recv_sem.at[0], sib).wait_send()

    landings = [
        (2 * zt + low, (zt * 16 + y * 4 + low + 2 * core, zh * 2 + (x + low + 1 + core) % 2)) for zt, low in spots
    ]
    home = z * 2 + x // 2
    first_hop = [
        remote(lvown.at[i], lvin.at[home], row_sem.at[0], row_sem.at[1], there) for i, there in landings
    ]
    for i, there in landings:
        for q in range(4):
            src = spec_ref.at[:, i, :, q * 256 : (q + 1) * 256]
            dst = g.at[home, y * 2 + x % 2, q]
            first_hop.append(remote(src, dst, own_send.at[0], own_recv.at[home, q], there))
    for copy in first_hop[8:24]:
        copy.start()
    loads[0].wait()

    def measure(i, carry):
        re = spec[0, i].astype(F32)
        im = spec[1, i].astype(F32)
        lvown[i] = jnp.sum(jnp.sqrt(re * re + im * im), axis=0, keepdims=True)
        return carry

    lax.fori_loop(0, 8, measure, 0)
    for copy in first_hop[:8]:
        copy.start()
    for copy in first_hop[24:]:
        copy.start()
    loads[1].wait()
    send(qown, qbuf, 0, 0, sib)

    acc[...] = jnp.zeros_like(acc)
    w[NEED] = jnp.zeros_like(w[NEED])

    def hop(gi, m, q, kind, there):
        block = g.at[gi, m, q]
        arrival = gsib.at[gi] if kind == 3 else grecv.at[gi, m // 2, q]
        return remote(block, block, gsend.at[kind], arrival, there)

    def needs(at):
        return at, jnp.minimum(at + 2, 3)

    def upward(at, relay):
        lone = needs(at)
        return jnp.where(relay, jnp.where(at == 3, 0, at), lone[0]), jnp.where(relay, 3, lone[1])

    def downward(at, relay):
        lone = needs(at)
        return jnp.where(relay, jnp.maximum(at - 1, 0), lone[0]), jnp.where(relay, 3, lone[1])

    above, below, beyond = (y + 1) % 4, (y + 3) % 4, (y + 2) % 4
    mine = needs(y)

    def group_of(n):
        k = n // 2
        zt = jnp.where(k == 0, zs[0], jnp.where(k == 1, zs[1], jnp.where(k == 2, zs[2], zs[3])))
        return zt * 2 + n % 2

    def whitened(gi, m, tile):
        cols = tile_at(tile)
        half = tile_at(tile % 2)
        re = g[gi, m, tile // 2, 0, :, half].astype(F32)
        im = g[gi, m, tile // 2, 1, :, half].astype(F32)
        factor = use_ref[:, cols] / (jnp.sqrt(re * re + im * im) + add_ref[:, cols])
        return (re * factor).astype(BF), (im * factor).astype(BF)

    def within(q, span):
        return (q >= span[0]) & (q <= span[1])

    def start_if(wanted, *args):
        @pl.when(wanted)
        def _():
            hop(*args).start()

    def own(n):
        gi = group_of(n)
        m = y * 2 + par
        even = n % 2 == 0

        def one(q, carry):
            block = g.at[gi, m, q]
            remote(block, block, own_send.at[0], own_recv.at[gi, q], sib).wait_recv()

            @pl.when(n >= RAW)
            def _():
                for h in range(2):
                    re, im = whitened(gi, m, q * 2 + h)
                    g[gi, m, q, 0, :, h * TILE : (h + 1) * TILE] = re
                    g[gi, m, q, 1, :, h * TILE : (h + 1) * TILE] = im

            start_if(within(q, upward(above, even)), gi, m, q, 0, up)
            start_if(within(q, downward(below, jnp.logical_not(even))), gi, m, q, 1, down)
            start_if(within(q, mine), gi, m, q, 3, sib)
            return carry

        lax.fori_loop(0, 4, one, 0)

    def relay(gi, m, span, passed, there):
        def one(q, carry):
            hop(gi, m, q, 0, sib).wait_recv()
            start_if(within(q, passed), gi, m, q, 2, there)
            start_if(within(q, mine), gi, m, q, 3, sib)
            return carry

        lax.fori_loop(span[0], span[1] + 1, one, 0)

    def near(n):
        gi = group_of(n)
        even = n % 2 == 0
        lone = needs(above)
        passed = jnp.where(even, lone[0], 4), lone[1]
        relay(gi, below * 2 + par, upward(y, even), passed, up)
        lone = needs(below)
        passed = jnp.where(even, 4, lone[0]), lone[1]
        relay(gi, above * 2 + par, downward(y, jnp.logical_not(even)), passed, down)

    def far(n):
        relay(group_of(n), beyond * 2 + par, mine, (4, 4), up)

    lane = lax.broadcasted_iota(jnp.int32, (FB, TILE), 1)

    def compute(n):
        gi = group_of(n)
        count = mine[1] - mine[0] + 1
        for size in (1, 2, 3):

            @pl.when(count == size)
            def _(size=size):
                block = g.at[gi, pl.ds(0, size)]
                remote(block, block, gsend.at[3], gsib.at[gi], sib).wait_recv()


        @pl.when(n < RAW)
        def _():
            def whiten(m, carry):
                for a in range(NEED):
                    re, im = whitened(gi, m, jnp.minimum(t + a, 7))
                    w[a, 0, m] = jnp.where(t + a < 8, re, jnp.zeros_like(re))
                    w[a, 1, m] = jnp.where(t + a < 8, im, jnp.zeros_like(im))
                return carry

            lax.fori_loop(0, 8, whiten, 0)

        @pl.when(n >= RAW)
        def _():
            for a in range(NEED):
                tile = jnp.minimum(t + a, 7)
                for part in range(2):
                    value = g[gi, :, tile // 2, part, :, tile_at(tile % 2)]
                    w[a, part] = jnp.where(t + a < 8, value, jnp.zeros_like(value))

        def cross(m, carry):
            rows = pl.ds(pl.multiple_of(m * FB, FB), FB)
            own_re = w[0, 0, m].astype(F32)
            own_im = w[0, 1, m].astype(F32)
            for j in range(NOFF):
                whole = off_ref[j] // 8
                rest = off_ref[j] % 8 * 16
                keep = lane >= rest
                back = (TILE - rest) % TILE
                far_re = jnp.where(keep, w[whole, 0, m].astype(F32), w[whole + 1, 0, m].astype(F32))
                far_im = jnp.where(keep, w[whole, 1, m].astype(F32), w[whole + 1, 1, m].astype(F32))
                far_re = pltpu.roll(far_re, back, 1)
                far_im = pltpu.roll(far_im, back, 1)
                xmat[rows, j * TILE : (j + 1) * TILE] = (own_re * far_re + own_im * far_im).astype(BF)
                xmat[rows, 512 + j * TILE : 512 + (j + 1) * TILE] = (own_im * far_re - own_re * far_im).astype(BF)
            return carry

        lax.fori_loop(0, 8, cross, 0)
        acc[...] += jnp.dot(tab[gi], xmat[...], preferred_element_type=F32)

    for n in range(4):
        own(n)
    near(0)
    near(1)
    near(2)
    remote(lvin, lvin, row_sem.at[0], row_sem.at[1], sib).wait_recv()
    part = lvin[0]
    for k in range(1, 8):
        part = part + lvin[k]
    lvall[t] = part
    for d in range(1, 8):
        send(lvall.at[t], lvall.at[t], 1, 1, t_peer(d))
    near(3)
    for n in range(4):
        far(n)
    received(qbuf, 0)
    row = pl.ds(2 * z + x % 2, 1)
    use_ref[...] = jnp.where(x // 2 == core, qown[row], qbuf[row]).astype(F32)
    received(lvall.at[pl.ds(0, 7)], 1)
    level = lvall[0]
    for n in range(1, 8):
        level = level + lvall[n]
    add_ref[...] = 0.5 * (level / F + 1e-05)
    loads[2].wait()

    def turn(i, carry):
        @pl.when(i < 4)
        def _():
            own(i + 4)

        @pl.when((i >= 1) & (i < 5))
        def _():
            near(i + 3)

        @pl.when((i >= 2) & (i < 6))
        def _():
            far(i + 2)

        compute(i)
        return carry

    lax.fori_loop(0, 8, turn, 0)

    scale = 1.0 / math.sqrt(F)

    def phases(j):
        left = tile_at(j)
        right = tile_at(j + NOFF)
        a = acc[:HALF, left]
        b = acc[HALF:, right]
        c = acc[HALF:, left]
        d = acc[:HALF, right]
        pos_r = (a - b) * scale
        neg_r = (a + b) * scale
        pos_q = (d + c) * scale
        neg_q = (d - c) * scale
        pos_p = pos_r * pos_r + pos_q * pos_q
        neg_p = neg_r * neg_r + neg_q * neg_q
        mean = jnp.sum(pos_p + neg_p, axis=0, keepdims=True) / LAGS
        floor = 0.25 * (mean + 1e-06)
        pos_d = jnp.sqrt(pos_p + floor)
        neg_d = jnp.sqrt(neg_p + floor)
        values = ((pos_r, pos_r / pos_d, pos_q / pos_d), (neg_r, neg_r / neg_d, neg_q / neg_d))
        for s in range(2):
            for part in range(3):
                rows = values[s][part].reshape(8, 2, 8, TILE)
                for h in range(2):
                    p[h, s, part, j] = rows[:, h].reshape(64, TILE)

    right, left, across = (x + 1) % 4, (x + 3) % 4, (x + 2) % 4

    def across_out(h):
        send(p.at[h, 0, :, across], ring.at[h, 0], 2, 2 + 6 * h, x_peer(1))
        send(p.at[h, 1, :, across], ring.at[h, 1], 2, 3 + 6 * h, x_peer(3))

    def plain_out(h):
        send(p.at[h, 1, :, right], ringin.at[h, 0], 3, 4 + 6 * h, x_peer(1))
        send(p.at[h, 0, :, left], ringin.at[h, 1], 3, 5 + 6 * h, x_peer(3))

    def both_out(h):
        received(ring.at[h, 0], 2 + 6 * h)
        ringsum[h, 0] = ring[h, 0] + p[h, 0, :, right]
        send(ringsum.at[h, 0], ringin.at[h, 2], 3, 6 + 6 * h, x_peer(1))
        received(ring.at[h, 1], 3 + 6 * h)
        ringsum[h, 1] = ring[h, 1] + p[h, 1, :, left]
        send(ringsum.at[h, 1], ringin.at[h, 3], 3, 7 + 6 * h, x_peer(3))

    def lag_rows(where):
        return pl.ds(pl.multiple_of(where * 8, 8), 8)

    def z_out(h):
        for n in range(4):
            received(ringin.at[h, n], 4 + 6 * h + n)
        zacc[h, 0] = (p[h, 0, :, x] + ringin[h, 1]) + ringin[h, 2]
        zacc[h, 1] = (p[h, 1, :, x] + ringin[h, 0]) + ringin[h, 3]
        for d in (4, 3, 5, 2, 6, 1, 7):
            send(zacc.at[h, :, :, lag_rows((zall + d) % 8)], zbuf.at[h, d - 1], 4 + h, 14 + h, z_peer(d))

    def z_in(h):
        received(zbuf.at[h], 14 + h)
        total = zacc[h, :, :, lag_rows(zall)]
        for d in range(7):
            total = total + zbuf[h, d]
        linear = total[:, 0] / WINDOWS
        real = total[:, 1] / WINDOWS
        imag = total[:, 2] / WINDOWS
        st[t, :, 8 * h : 8 * h + 8] = linear * (real * real + imag * imag)

    phases(across)
    across_out(0)
    phases(right)
    phases(left)
    plain_out(0)
    across_out(1)
    phases(x)
    both_out(0)
    plain_out(1)
    both_out(1)
    z_out(0)
    z_out(1)
    z_in(0)
    z_in(1)

    for d in range(1, 8):
        send(st.at[t], st.at[t], 6, 16, t_peer(d))
    received(st.at[pl.ds(0, 7)], 16)
    shift = off_ref[x]
    whole = shift // 8
    rest = shift % 8 * 16
    wide = lax.broadcasted_iota(jnp.int32, (2, 16, TILE), 2)
    pieces = []
    for n in range(4):
        tile = 2 * n + y // 2
        first = tile - whole
        a = jnp.where(first >= 0, st[jnp.maximum(first, 0)], 0.0)
        b = jnp.where(first >= 1, st[jnp.maximum(first - 1, 0)], 0.0)
        rev = pltpu.roll(jnp.where(wide < TILE - rest, a, b).reshape(32, TILE), rest, 1).reshape(2, 16, TILE)
        ahead = st[tile]
        pieces.append(ahead[0] + rev[1])
        pieces.append(ahead[1] + rev[0])
    tbuf[...] = jnp.concatenate(pieces, axis=0).T

    def channel_rows(where):
        return pl.ds(pl.multiple_of(y % 2 * 64 + where * 16, 16), 16)

    for d in (1, 2, 3):
        send(tbuf.at[channel_rows((x + d) % 4)], jbuf.at[x], 7, 17, x_peer(d))
    jbuf[x] = tbuf[channel_rows(x)]
    received(jbuf.at[pl.ds(0, 3)], 17)
    group = lax.broadcasted_iota(jnp.int32, (16, TILE), 1) // 32
    for n in range(4):
        merged = jnp.zeros((16, TILE), F32)
        for j in range(NOFF):
            merged = jnp.where(group == j, pltpu.roll(jbuf[j], (32 * (j - n)) % TILE, 1), merged)
        mbuf[n] = merged
    for d in (4, 3, 5, 2, 6, 1, 7):
        send(mbuf.at[(zall + d) % 4], rbuf.at[zall], 8, 18, z_peer(d))
    rbuf[zall] = mbuf[zall % 4]
    received(rbuf.at[pl.ds(0, 7)], 18)
    spot = lax.broadcasted_iota(jnp.int32, (16, TILE), 1)
    span = spot // 16
    for j in range(NOFF):
        for s in range(2):
            merged = jnp.zeros((16, TILE), F32)
            for n in range(8):
                at = 7 - n if s else n
                merged = jnp.where(span == at, pltpu.roll(rbuf[n], (16 * at - 32 * j - 16 * s) % TILE, 1), merged)
            if s:
                for bit in (1, 2, 4, 8):
                    merged = jnp.where(
                        spot // bit % 2 == 1, pltpu.roll(merged, bit, 1), pltpu.roll(merged, TILE - bit, 1)
                    )
            out_ref[:, j, (1 - s) * HALF : (2 - s) * HALF] = merged

    gone(lvown, row_sem.at[0])
    gone(g.at[0], own_send.at[0])
    gone(qown, send_sem.at[0])
    gone(lvall.at[pl.ds(0, 7)], send_sem.at[1])
    gone(ring, send_sem.at[2])
    gone(ringin, send_sem.at[3])
    for h in range(2):
        gone(zbuf.at[h], send_sem.at[4 + h])
    gone(st.at[pl.ds(0, 7)], send_sem.at[6])
    gone(jbuf.at[pl.ds(0, 3)], send_sem.at[7])
    gone(rbuf.at[pl.ds(0, 7)], send_sem.at[8])
    width = (3, 3, 2, 1)
    for at in range(4):
        ahead, behind = (at + 1) % 4, (at + 3) % 4
        upper = (4, 3, 2, 4)[ahead]
        lower = (4, 4, 3, 2)[behind]

        @pl.when(y == at)
        def _(at=at, ahead=ahead, behind=behind, upper=upper, lower=lower):
            gone(g.at[0, pl.ds(0, upper + width[ahead])], gsend.at[0])
            gone(g.at[0, pl.ds(0, lower + width[behind])], gsend.at[1])
            gone(g.at[0, pl.ds(0, width[ahead] + width[behind])], gsend.at[2])
            gone(g.at[pl.ds(0, width[at])], gsend.at[3])


def whole_window(offsets, spectra, quality, table):
    vmem = pl.BlockSpec(memory_space=pltpu.VMEM)
    return pl.pallas_call(
        window_kernel,
        name="whole_window",
        out_shape=jax.ShapeDtypeStruct((16, NOFF, LAGS), F32),
        in_specs=[pl.BlockSpec(memory_space=pltpu.SMEM)] + [pl.BlockSpec(memory_space=pl.ANY)] * 3,
        out_specs=vmem,
        scratch_shapes=[
            pltpu.VMEM((2, 8, FB, NCH), BF),
            pltpu.VMEM((8, NCH), jnp.int32),
            pltpu.VMEM((8, NCH), jnp.int32),
            pltpu.VMEM((8, 2 * HALF, GROUP), BF),
            pltpu.VMEM((8, 8, 4, 2, FB, 256), BF),
            pltpu.VMEM((8, 1, NCH), F32),
            pltpu.VMEM((8, 1, NCH), F32),
            pltpu.VMEM((8, 1, NCH), F32),
            pltpu.VMEM((1, NCH), F32),
            pltpu.VMEM((1, NCH), F32),
            pltpu.VMEM((NEED + 1, 2, 8, FB, TILE), BF),
            pltpu.VMEM((GROUP, 2 * NOFF * TILE), BF),
            pltpu.VMEM((2 * HALF, 2 * NOFF * TILE), F32),
            pltpu.VMEM((2, 2, 3, NOFF, 64, TILE), F32),
            pltpu.VMEM((2, 2, 3, 64, TILE), F32),
            pltpu.VMEM((2, 2, 3, 64, TILE), F32),
            pltpu.VMEM((2, 4, 3, 64, TILE), F32),
            pltpu.VMEM((2, 2, 3, 64, TILE), F32),
            pltpu.VMEM((2, 7, 2, 3, 8, TILE), F32),
            pltpu.VMEM((8, 2, 16, TILE), F32),
            pltpu.VMEM((TILE, TILE), F32),
            pltpu.VMEM((NOFF, 16, TILE), F32),
            pltpu.VMEM((4, 16, TILE), F32),
            pltpu.VMEM((8, 16, TILE), F32),
            pltpu.SemaphoreType.DMA((3,)),
            pltpu.SemaphoreType.DMA((8, 4)),
            pltpu.SemaphoreType.DMA((1,)),
            pltpu.SemaphoreType.DMA((2,)),
            pltpu.SemaphoreType.DMA((4,)),
            pltpu.SemaphoreType.DMA((8, 4, 4)),
            pltpu.SemaphoreType.DMA((8,)),
            pltpu.SemaphoreType.DMA((9,)),
            pltpu.SemaphoreType.DMA((19,)),
        ],
        compiler_params=pltpu.CompilerParams(collective_id=0, has_side_effects=True),
    )(offsets, spectra, quality, table)


def shards(spectra, quality, offsets):
    table = jnp.asarray(half_table()).astype(BF)
    return whole_window(offsets, spectra, quality, table)


def solution(mesh):
    return jax.shard_map(
        shards,
        mesh=mesh,
        in_specs=(P(None, "tm", "chan", None), P("tm", None), P()),
        out_specs=P("chan", None, None),
        check_vma=False,
    )
```

time: 104 us -> 95.3 us (0.916)
  Pallas kernels: 102 us -> 93.7 us
    pallas_call x1, Pallas kernels: 102 us -> 93.7 us  [whole_window(): pl.pallas_call(window_kernel, name='whole_window', out_shape=jax.ShapeDty...]
    unnamed x0 -> x1, local copies, waits for them, and re-layouts: none -> 1.47 us
where the time goes in v4:
time: 95.3 us; the launch traced here: 95.2 us
  Pallas kernels  93.7 us (98%)
  local copies, waits for them, and re-layouts  1.47 us (2%)
    pallas_call x1, Pallas kernels, whole_window(): pl.pallas_call(window_kernel, name='whole_window', out_shape=jax.ShapeDty...  93.7 us

profile of v4, /device:TPU:1, one launch (start us, length us, event | category | flops | bytes accessed | tf_op | source)
XLA Modules:
  0.0 95.2 jit_solution(14865189938955043389)
XLA Ops:
  0.0 93.7 %whole_window.1 = f32[16,4,256]{2,1,0:T(4,128)} custom-call(s32[4]{0:T(128)} %off_ref.1, bf16[2,8,32,1024]{3,2,1,0:T(8,128)(2,1)} %spec_ref.1, s32[8,1024]{1,0:T(8,128)} %qual_ref.1, bf16[8,256,256]{2,1,0:T(8,128)(2,1)} %constant.4.tab_hbm), custom_call_target="tpu_custom_call" | custom-call | tf_op jit(solution)/shard_map/whole_window/pallas_call | solution.py:476
  93.7 1.5 %copy.6 = f32[16,4,256]{2,1,0:T(4,128)} copy(f32[16,4,256]{2,1,0:T(4,128)} %whole_window.1) | data formatting | bytes 131072

commit v5 on v4

--- a/solution.py
+++ b/solution.py
@@ -242,7 +242,7 @@
                     w[a, 1, m] = jnp.where(t + a < 8, im, jnp.zeros_like(im))
                 return carry
 
-            lax.fori_loop(0, 8, whiten, 0)
+            lax.fori_loop(0, 8, whiten, 0, unroll=4)
 
         @pl.when(n >= RAW)
         def _():
@@ -269,7 +269,7 @@
                 xmat[rows, 512 + j * TILE : 512 + (j + 1) * TILE] = (own_im * far_re - own_re * far_im).astype(BF)
             return carry
 
-        lax.fori_loop(0, 8, cross, 0)
+        lax.fori_loop(0, 8, cross, 0, unroll=8)
         acc[...] += jnp.dot(tab[gi], xmat[...], preferred_element_type=F32)
 
     for n in range(4):
@@ -378,7 +378,9 @@
         linear = total[:, 0] / WINDOWS
         real = total[:, 1] / WINDOWS
         imag = total[:, 2] / WINDOWS
-        st[t, :, 8 * h : 8 * h + 8] = linear * (real * real + imag * imag)
+        st[h, t] = linear * (real * real + imag * imag)
+        for d in range(1, 8):
+            send(st.at[h, t], st.at[h, t], 6, 16 + h, t_peer(d))
 
     phases(across)
     across_out(0)
@@ -395,32 +397,35 @@
     z_in(0)
     z_in(1)
 
-    for d in range(1, 8):
-        send(st.at[t], st.at[t], 6, 16, t_peer(d))
-    received(st.at[pl.ds(0, 7)], 16)
+    for h in range(2):
+        received(st.at[h, pl.ds(0, 7)], 16 + h)
     shift = off_ref[x]
     whole = shift // 8
     rest = shift % 8 * 16
-    wide = lax.broadcasted_iota(jnp.int32, (2, 16, TILE), 2)
+    wide = lax.broadcasted_iota(jnp.int32, (32, TILE), 1)
+
+    def stack(tile):
+        return jnp.concatenate([st[h, tile, s] for s in range(2) for h in range(2)], axis=0)
+
     pieces = []
     for n in range(4):
         tile = 2 * n + y // 2
         first = tile - whole
-        a = jnp.where(first >= 0, st[jnp.maximum(first, 0)], 0.0)
-        b = jnp.where(first >= 1, st[jnp.maximum(first - 1, 0)], 0.0)
-        rev = pltpu.roll(jnp.where(wide < TILE - rest, a, b).reshape(32, TILE), rest, 1).reshape(2, 16, TILE)
-        ahead = st[tile]
-        pieces.append(ahead[0] + rev[1])
-        pieces.append(ahead[1] + rev[0])
+        a = jnp.where(first >= 0, stack(jnp.maximum(first, 0)), 0.0)
+        b = jnp.where(first >= 1, stack(jnp.maximum(first - 1, 0)), 0.0)
+        rev = pltpu.roll(jnp.where(wide < TILE - rest, a, b), rest, 1)
+        ahead = stack(tile)
+        pieces.append(ahead[:16] + rev[16:])
+        pieces.append(ahead[16:] + rev[:16])
     tbuf[...] = jnp.concatenate(pieces, axis=0).T
 
     def channel_rows(where):
         return pl.ds(pl.multiple_of(y % 2 * 64 + where * 16, 16), 16)
 
     for d in (1, 2, 3):
-        send(tbuf.at[channel_rows((x + d) % 4)], jbuf.at[x], 7, 17, x_peer(d))
+        send(tbuf.at[channel_rows((x + d) % 4)], jbuf.at[x], 7, 18, x_peer(d))
     jbuf[x] = tbuf[channel_rows(x)]
-    received(jbuf.at[pl.ds(0, 3)], 17)
+    received(jbuf.at[pl.ds(0, 3)], 18)
     group = lax.broadcasted_iota(jnp.int32, (16, TILE), 1) // 32
     for n in range(4):
         merged = jnp.zeros((16, TILE), F32)
@@ -428,9 +433,9 @@
             merged = jnp.where(group == j, pltpu.roll(jbuf[j], (32 * (j - n)) % TILE, 1), merged)
         mbuf[n] = merged
     for d in (4, 3, 5, 2, 6, 1, 7):
-        send(mbuf.at[(zall + d) % 4], rbuf.at[zall], 8, 18, z_peer(d))
+        send(mbuf.at[(zall + d) % 4], rbuf.at[zall], 8, 19, z_peer(d))
     rbuf[zall] = mbuf[zall % 4]
-    received(rbuf.at[pl.ds(0, 7)], 18)
+    received(rbuf.at[pl.ds(0, 7)], 19)
     spot = lax.broadcasted_iota(jnp.int32, (16, TILE), 1)
     span = spot // 16
     for j in range(NOFF):
@@ -454,7 +459,7 @@
     gone(ringin, send_sem.at[3])
     for h in range(2):
         gone(zbuf.at[h], send_sem.at[4 + h])
-    gone(st.at[pl.ds(0, 7)], send_sem.at[6])
+    gone(st.at[:, pl.ds(0, 7)], send_sem.at[6])
     gone(jbuf.at[pl.ds(0, 3)], send_sem.at[7])
     gone(rbuf.at[pl.ds(0, 7)], send_sem.at[8])
     width = (3, 3, 2, 1)
@@ -499,7 +504,7 @@
             pltpu.VMEM((2, 4, 3, 64, TILE), F32),
             pltpu.VMEM((2, 2, 3, 64, TILE), F32),
             pltpu.VMEM((2, 7, 2, 3, 8, TILE), F32),
-            pltpu.VMEM((8, 2, 16, TILE), F32),
+            pltpu.VMEM((2, 8, 2, 8, TILE), F32),
             pltpu.VMEM((TILE, TILE), F32),
             pltpu.VMEM((NOFF, 16, TILE), F32),
             pltpu.VMEM((4, 16, TILE), F32),
@@ -512,7 +517,7 @@
             pltpu.SemaphoreType.DMA((8, 4, 4)),
             pltpu.SemaphoreType.DMA((8,)),
             pltpu.SemaphoreType.DMA((9,)),
-            pltpu.SemaphoreType.DMA((19,)),
+            pltpu.SemaphoreType.DMA((20,)),
         ],
         compiler_params=pltpu.CompilerParams(collective_id=0, has_side_effects=True),
     )(offsets, spectra, quality, table)

time: 95.3 us -> 92.9 us (0.975)
  Pallas kernels: 93.7 us -> 91.3 us
    pallas_call x1, Pallas kernels: 93.7 us -> 91.3 us  [whole_window(): pl.pallas_call(window_kernel, name='whole_window', out_shape=jax.ShapeDty...]
where the time goes in v5:
time: 92.9 us; the launch traced here: 92.8 us
  Pallas kernels  91.3 us (98%)
  local copies, waits for them, and re-layouts  1.47 us (2%)
    pallas_call x1, Pallas kernels, whole_window(): pl.pallas_call(window_kernel, name='whole_window', out_shape=jax.ShapeDty...  91.3 us

profile of v5, /device:TPU:1, one launch (start us, length us, event | category | flops | bytes accessed | tf_op | source)
XLA Modules:
  0.0 92.8 jit_solution(6529742235133994164)
XLA Ops:
  0.0 91.3 %whole_window.1 = f32[16,4,256]{2,1,0:T(4,128)} custom-call(s32[4]{0:T(128)} %off_ref.1, bf16[2,8,32,1024]{3,2,1,0:T(8,128)(2,1)} %spec_ref.1, s32[8,1024]{1,0:T(8,128)} %qual_ref.1, bf16[8,256,256]{2,1,0:T(8,128)(2,1)} %constant.4.tab_hbm), custom_call_target="tpu_custom_call" | custom-call | tf_op jit(solution)/shard_map/whole_window/pallas_call | solution.py:481
  91.3 1.5 %copy.6 = f32[16,4,256]{2,1,0:T(4,128)} copy(f32[16,4,256]{2,1,0:T(4,128)} %whole_window.1) | data formatting | bytes 131072

commit v6 on v5

--- a/solution.py
+++ b/solution.py
@@ -45,7 +45,7 @@
 def window_kernel(
     off_ref, spec_ref, qual_ref, tab_hbm, out_ref,
     spec, qown, qbuf, tab, g, lvown, lvin, lvall, add_ref, use_ref, w, xmat, acc, p,
-    ring, ringsum, ringin, zacc, zbuf, st, tbuf, jbuf, mbuf, rbuf,
+    pair, ring, ringsum, ringin, zacc, zbuf, st, tbuf, jbuf, mbuf, rbuf,
     local_sem, own_recv, own_send, row_sem, gsend, grecv, gsib, send_sem, recv_sem,
 ):
     z, y, x, zh, core = place()
@@ -328,45 +328,62 @@
         neg_r = (a + b) * scale
         pos_q = (d + c) * scale
         neg_q = (d - c) * scale
-        pos_p = pos_r * pos_r + pos_q * pos_q
-        neg_p = neg_r * neg_r + neg_q * neg_q
-        mean = jnp.sum(pos_p + neg_p, axis=0, keepdims=True) / LAGS
+        power = (pos_r * pos_r + pos_q * pos_q) + (neg_r * neg_r + neg_q * neg_q)
+        mean = jnp.sum(power, axis=0, keepdims=True) / LAGS
         floor = 0.25 * (mean + 1e-06)
-        pos_d = jnp.sqrt(pos_p + floor)
-        neg_d = jnp.sqrt(neg_p + floor)
-        values = ((pos_r, pos_r / pos_d, pos_q / pos_d), (neg_r, neg_r / neg_d, neg_q / neg_d))
+
+        def halves(value):
+            rows = value.reshape(8, 2, 8, TILE)
+            return [rows[:, h].reshape(64, TILE) for h in range(2)]
+
+        return floor, ((halves(pos_r), halves(pos_q)), (halves(neg_r), halves(neg_q)))
+
+    def phasors(real, imag, floor):
+        depth = jnp.sqrt((real * real + imag * imag) + floor)
+        return real, real / depth, imag / depth
+
+    def keep_pair(found, s, k):
+        floor, values = found
+        for h in range(2):
+            pair[h, s, k, :64] = values[s][0][h]
+            pair[h, s, k, 64:128] = values[s][1][h]
+            pair[h, s, k, 128:] = jnp.broadcast_to(floor, (8, TILE))
+
+    def keep_full(found, s, k):
+        floor, values = found
+        for h in range(2):
+            for part, value in enumerate(phasors(values[s][0][h], values[s][1][h], floor)):
+                p[h, s, k, part] = value
+
+    def opened(h, n):
+        return phasors(ring[h, n, :64], ring[h, n, 64:128], ring[h, n, 128:129])
+
+    right, left, across = (x + 1) % 4, (x + 3) % 4, (x + 2) % 4
+
+    def across_out(h):
+        send(pair.at[h, 0, 0], ring.at[h, 0], 2, 2 + 6 * h, x_peer(1))
+        send(pair.at[h, 1, 0], ring.at[h, 1], 2, 3 + 6 * h, x_peer(3))
+
+    def plain_out(h):
+        send(pair.at[h, 1, 1], ring.at[h, 2], 2, 4 + 6 * h, x_peer(1))
+        send(pair.at[h, 0, 1], ring.at[h, 3], 2, 5 + 6 * h, x_peer(3))
+
+    def both_out(h):
         for s in range(2):
-            for part in range(3):
-                rows = values[s][part].reshape(8, 2, 8, TILE)
-                for h in range(2):
-                    p[h, s, part, j] = rows[:, h].reshape(64, TILE)
-
-    right, left, across = (x + 1) % 4, (x + 3) % 4, (x + 2) % 4
-
-    def across_out(h):
-        send(p.at[h, 0, :, across], ring.at[h, 0], 2, 2 + 6 * h, x_peer(1))
-        send(p.at[h, 1, :, across], ring.at[h, 1], 2, 3 + 6 * h, x_peer(3))
-
-    def plain_out(h):
-        send(p.at[h, 1, :, right], ringin.at[h, 0], 3, 4 + 6 * h, x_peer(1))
-        send(p.at[h, 0, :, left], ringin.at[h, 1], 3, 5 + 6 * h, x_peer(3))
-
-    def both_out(h):
-        received(ring.at[h, 0], 2 + 6 * h)
-        ringsum[h, 0] = ring[h, 0] + p[h, 0, :, right]
-        send(ringsum.at[h, 0], ringin.at[h, 2], 3, 6 + 6 * h, x_peer(1))
-        received(ring.at[h, 1], 3 + 6 * h)
-        ringsum[h, 1] = ring[h, 1] + p[h, 1, :, left]
-        send(ringsum.at[h, 1], ringin.at[h, 3], 3, 7 + 6 * h, x_peer(3))
+            received(ring.at[h, s], 2 + 6 * h + s)
+            for part, value in enumerate(opened(h, s)):
+                ringsum[h, s, part] = value + p[h, s, 1, part]
+            send(ringsum.at[h, s], ringin.at[h, s], 3, 6 + 6 * h + s, x_peer(3 if s else 1))
 
     def lag_rows(where):
         return pl.ds(pl.multiple_of(where * 8, 8), 8)
 
     def z_out(h):
-        for n in range(4):
-            received(ringin.at[h, n], 4 + 6 * h + n)
-        zacc[h, 0] = (p[h, 0, :, x] + ringin[h, 1]) + ringin[h, 2]
-        zacc[h, 1] = (p[h, 1, :, x] + ringin[h, 0]) + ringin[h, 3]
+        for s in range(2):
+            received(ring.at[h, 3 - s], 5 + 6 * h - s)
+            received(ringin.at[h, s], 6 + 6 * h + s)
+            for part, value in enumerate(opened(h, 3 - s)):
+                zacc[h, s, part] = (p[h, s, 0, part] + value) + ringin[h, s, part]
         for d in (4, 3, 5, 2, 6, 1, 7):
             send(zacc.at[h, :, :, lag_rows((zall + d) % 8)], zbuf.at[h, d - 1], 4 + h, 14 + h, z_peer(d))
 
@@ -382,13 +399,21 @@
         for d in range(1, 8):
             send(st.at[h, t], st.at[h, t], 6, 16 + h, t_peer(d))
 
-    phases(across)
+    found = phases(across)
+    keep_pair(found, 0, 0)
+    keep_pair(found, 1, 0)
     across_out(0)
-    phases(right)
-    phases(left)
+    onward = phases(right)
+    keep_pair(onward, 1, 1)
+    back = phases(left)
+    keep_pair(back, 0, 1)
     plain_out(0)
     across_out(1)
-    phases(x)
+    keep_full(onward, 0, 1)
+    keep_full(back, 1, 1)
+    found = phases(x)
+    keep_full(found, 0, 0)
+    keep_full(found, 1, 0)
     both_out(0)
     plain_out(1)
     both_out(1)
@@ -498,10 +523,11 @@
             pltpu.VMEM((NEED + 1, 2, 8, FB, TILE), BF),
             pltpu.VMEM((GROUP, 2 * NOFF * TILE), BF),
             pltpu.VMEM((2 * HALF, 2 * NOFF * TILE), F32),
-            pltpu.VMEM((2, 2, 3, NOFF, 64, TILE), F32),
+            pltpu.VMEM((2, 2, 2, 3, 64, TILE), F32),
+            pltpu.VMEM((2, 2, 2, 136, TILE), F32),
+            pltpu.VMEM((2, 4, 136, TILE), F32),
             pltpu.VMEM((2, 2, 3, 64, TILE), F32),
             pltpu.VMEM((2, 2, 3, 64, TILE), F32),
-            pltpu.VMEM((2, 4, 3, 64, TILE), F32),
             pltpu.VMEM((2, 2, 3, 64, TILE), F32),
             pltpu.VMEM((2, 7, 2, 3, 8, TILE), F32),
             pltpu.VMEM((2, 8, 2, 8, TILE), F32),

time: 92.9 us -> 91.3 us (0.983)
  Pallas kernels: 91.3 us -> 89.7 us
    pallas_call x1, Pallas kernels: 91.3 us -> 89.7 us  [whole_window(): pl.pallas_call(window_kernel, name='whole_window', out_shape=jax.ShapeDty...]
where the time goes in v6:
time: 91.3 us; the launch traced here: 91.2 us
  Pallas kernels  89.7 us (98%)
  local copies, waits for them, and re-layouts  1.47 us (2%)
    pallas_call x1, Pallas kernels, whole_window(): pl.pallas_call(window_kernel, name='whole_window', out_shape=jax.ShapeDty...  89.7 us

profile of v6, /device:TPU:1, one launch (start us, length us, event | category | flops | bytes accessed | tf_op | source)
XLA Modules:
  0.0 91.2 jit_solution(4978290534128757689)
XLA Ops:
  0.0 89.7 %whole_window.1 = f32[16,4,256]{2,1,0:T(4,128)} custom-call(s32[4]{0:T(128)} %off_ref.1, bf16[2,8,32,1024]{3,2,1,0:T(8,128)(2,1)} %spec_ref.1, s32[8,1024]{1,0:T(8,128)} %qual_ref.1, bf16[8,256,256]{2,1,0:T(8,128)(2,1)} %constant.4.tab_hbm), custom_call_target="tpu_custom_call" | custom-call | tf_op jit(solution)/shard_map/whole_window/pallas_call | solution.py:506
  89.7 1.5 %copy.6 = f32[16,4,256]{2,1,0:T(4,128)} copy(f32[16,4,256]{2,1,0:T(4,128)} %whole_window.1) | data formatting | bytes 131072

commit v7 on v6

--- a/solution.py
+++ b/solution.py
@@ -46,7 +46,7 @@
     off_ref, spec_ref, qual_ref, tab_hbm, out_ref,
     spec, qown, qbuf, tab, g, lvown, lvin, lvall, add_ref, use_ref, w, xmat, acc, p,
     pair, ring, ringsum, ringin, zacc, zbuf, st, tbuf, jbuf, mbuf, rbuf,
-    local_sem, own_recv, own_send, row_sem, gsend, grecv, gsib, send_sem, recv_sem,
+    local_sem, own_send, row_sem, gsend, grecv, gsib, send_sem, recv_sem,
 ):
     z, y, x, zh, core = place()
     chan = z * 16 + y * 4 + x
@@ -113,7 +113,7 @@
         for q in range(4):
             src = spec_ref.at[:, i, :, q * 256 : (q + 1) * 256]
             dst = g.at[home, y * 2 + x % 2, q]
-            first_hop.append(remote(src, dst, own_send.at[0], own_recv.at[home, q], there))
+            first_hop.append(remote(src, dst, own_send.at[0], grecv.at[home, y, q], there))
     for copy in first_hop[8:24]:
         copy.start()
     loads[0].wait()
@@ -182,7 +182,7 @@
 
         def one(q, carry):
             block = g.at[gi, m, q]
-            remote(block, block, own_send.at[0], own_recv.at[gi, q], sib).wait_recv()
+            remote(block, block, own_send.at[0], grecv.at[gi, y, q], sib).wait_recv()
 
             @pl.when(n >= RAW)
             def _():
@@ -411,11 +411,11 @@
     across_out(1)
     keep_full(onward, 0, 1)
     keep_full(back, 1, 1)
+    both_out(0)
+    plain_out(1)
     found = phases(x)
     keep_full(found, 0, 0)
     keep_full(found, 1, 0)
-    both_out(0)
-    plain_out(1)
     both_out(1)
     z_out(0)
     z_out(1)
@@ -474,7 +474,7 @@
                     merged = jnp.where(
                         spot // bit % 2 == 1, pltpu.roll(merged, bit, 1), pltpu.roll(merged, TILE - bit, 1)
                     )
-            out_ref[:, j, (1 - s) * HALF : (2 - s) * HALF] = merged
+            out_ref[1 - s, j] = merged
 
     gone(lvown, row_sem.at[0])
     gone(g.at[0], own_send.at[0])
@@ -506,7 +506,7 @@
     return pl.pallas_call(
         window_kernel,
         name="whole_window",
-        out_shape=jax.ShapeDtypeStruct((16, NOFF, LAGS), F32),
+        out_shape=jax.ShapeDtypeStruct((2, NOFF, 16, HALF), F32),
         in_specs=[pl.BlockSpec(memory_space=pltpu.SMEM)] + [pl.BlockSpec(memory_space=pl.ANY)] * 3,
         out_specs=vmem,
         scratch_shapes=[
@@ -536,7 +536,6 @@
             pltpu.VMEM((4, 16, TILE), F32),
             pltpu.VMEM((8, 16, TILE), F32),
             pltpu.SemaphoreType.DMA((3,)),
-            pltpu.SemaphoreType.DMA((8, 4)),
             pltpu.SemaphoreType.DMA((1,)),
             pltpu.SemaphoreType.DMA((2,)),
             pltpu.SemaphoreType.DMA((4,)),
@@ -551,7 +550,8 @@
 
 def shards(spectra, quality, offsets):
     table = jnp.asarray(half_table()).astype(BF)
-    return whole_window(offsets, spectra, quality, table)
+    halves = whole_window(offsets, spectra, quality, table)
+    return jnp.transpose(halves, (2, 1, 0, 3)).reshape(16, NOFF, LAGS)
 
 
 def solution(mesh):

time: 91.3 us -> 91.1 us (level)
    reshape x0 -> x2, local copies, waits for them, and re-layouts: none -> 1.59 us  [shards(): return jnp.transpose(halves, (2, 1, 0, 3)).reshape(16, NOFF, LAGS)]
    unnamed x1 -> x0, local copies, waits for them, and re-layouts: 1.47 us -> none
where the time goes in v7:
time: 91.1 us; the launch traced here: 91 us
  Pallas kernels  89.4 us (98%)
  local copies, waits for them, and re-layouts  1.59 us (2%)
    pallas_call x1, Pallas kernels, whole_window(): pl.pallas_call(window_kernel, name='whole_window', out_shape=jax.ShapeDty...  89.4 us

profile of v7, /device:TPU:1, one launch (start us, length us, event | category | flops | bytes accessed | tf_op | source)
XLA Modules:
  0.0 91.0 jit_solution(4245635211036342424)
XLA Ops:
  0.0 89.4 %whole_window.1 = f32[2,4,16,128]{3,2,1,0:T(8,128)} custom-call(s32[4]{0:T(128)} %off_ref.1, bf16[2,8,32,1024]{3,2,1,0:T(8,128)(2,1)} %spec_ref.1, s32[8,1024]{1,0:T(8,128)} %qual_ref.1, bf16[8,256,256]{2,1,0:T(8,128)(2,1)} %constant.4.tab_hbm), custom_call_target="tpu_custom_call" | custom-call | tf_op jit(solution)/shard_map/whole_window/pallas_call | solution.py:506
  89.4 0.9 copy.7
  90.3 0.7 reshape.4

commit v8 on v7

--- a/solution.py
+++ b/solution.py
@@ -124,7 +124,7 @@
         lvown[i] = jnp.sum(jnp.sqrt(re * re + im * im), axis=0, keepdims=True)
         return carry
 
-    lax.fori_loop(0, 8, measure, 0)
+    lax.fori_loop(0, 8, measure, 0, unroll=4)
     for copy in first_hop[:8]:
         copy.start()
     for copy in first_hop[24:]:
@@ -242,7 +242,7 @@
                     w[a, 1, m] = jnp.where(t + a < 8, im, jnp.zeros_like(im))
                 return carry
 
-            lax.fori_loop(0, 8, whiten, 0, unroll=4)
+            lax.fori_loop(0, 8, whiten, 0, unroll=8)
 
         @pl.when(n >= RAW)
         def _():

time: 91.1 us -> 91.1 us (level)
  no operation moved by 1% of the time
where the time goes in v8:
time: 91.1 us; the launch traced here: 91 us
  Pallas kernels  89.4 us (98%)
  local copies, waits for them, and re-layouts  1.59 us (2%)
    pallas_call x1, Pallas kernels, whole_window(): pl.pallas_call(window_kernel, name='whole_window', out_shape=jax.ShapeDty...  89.4 us

profile of v8, /device:TPU:1, one launch (start us, length us, event | category | flops | bytes accessed | tf_op | source)
XLA Modules:
  0.0 91.0 jit_solution(11151498870704218680)
XLA Ops:
  0.0 89.4 %whole_window.1 = f32[2,4,16,128]{3,2,1,0:T(8,128)} custom-call(s32[4]{0:T(128)} %off_ref.1, bf16[2,8,32,1024]{3,2,1,0:T(8,128)(2,1)} %spec_ref.1, s32[8,1024]{1,0:T(8,128)} %qual_ref.1, bf16[8,256,256]{2,1,0:T(8,128)(2,1)} %constant.4.tab_hbm), custom_call_target="tpu_custom_call" | custom-call | tf_op jit(solution)/shard_map/whole_window/pallas_call | solution.py:506
  89.4 0.9 copy.7
  90.3 0.7 reshape.4
